TPU v7x, 768 devices: a whole 4x8x12 slice. The times are simulated.
768 devices in a mesh: node: 48 (over x_hi, z, core), rep: 16 (over y, x_lo).
Axes of the slice: x: 4 (x_hi: 2, x_lo: 2; x = x_hi * 2 + x_lo), y: 8, z: 12, core: 2. Of those that a mesh axis runs over, the one named last changes fastest.
Arguments:
- aggregated: bfloat16 [196608, 512], P(('node', 'rep')), may hold values from -6 to 6
- cotangent: bfloat16 [196608, 512], P(('node', 'rep')), may hold values from -6 to 6
- kernel_in: bfloat16 [512, 2048], P(None, 'rep'), may hold values from -0.25 to 0.25
- kernel_out: bfloat16 [2048, 512], P('rep'), may hold values from -0.125 to 0.125
- tile_values: bfloat16 [768, 4, 256, 256], P(('node', 'rep')), may hold values from -0.5 to 0.5
- tile_cols: int32 [768, 4], P(('node', 'rep')), may hold values from 0 to 2, as said below
- tile_count: int32 [768], P(('node', 'rep')), may hold values from 1 to 4, as said below
Outputs:
- grad_nodes: bfloat16 [196608, 512], P(('node', 'rep'))
- grad_in: float32 [512, 2048], P(None, 'rep')
- grad_out: float32 [2048, 512], P('rep')
Inputs may be any that keep to these rules, and one draw needn't show every extreme that they name: tile_cols 0, 1 and 2 name the block of the previous cycle position with the same rep index, the block itself and that of the next cycle position; slots at or past tile_count are ignored. `tile_count`: some block row has all 4 slots live.
All inputs are finite; a program needn't handle non-finite values.
Results may differ from a plain program's by a relative error of at most 0.024.
Values may be sent and summed in bfloat16 or wider, within the bound.
A program may use at most 64 MiB of HBM per device.

v0:
```python
import math

import jax
import jax.numpy as jnp
from jax import lax
from jax.sharding import PartitionSpec as P


def with_halo(block, sides, width):
    for axis, dim in sides:
        count = lax.axis_size(axis)
        forward = [(i, i + 1) for i in range(count - 1)]
        forward.append((count - 1, 0))
        backward = [(target, source) for source, target in forward]
        low = lax.ppermute(
            lax.slice_in_dim(block, block.shape[dim] - width, None, axis=dim), axis, forward
        )
        high = lax.ppermute(lax.slice_in_dim(block, 0, width, axis=dim), axis, backward)
        block = jnp.concatenate([low, block, high], axis=dim)
    return block


def gelu_value(pre_act):
    inner = math.sqrt(2.0 / math.pi) * (pre_act + 0.044715 * pre_act * pre_act * pre_act)
    return 0.5 * pre_act * (1.0 + jnp.tanh(inner))


def gelu_slope(pre_act):
    inner = math.sqrt(2.0 / math.pi) * (pre_act + 0.044715 * pre_act * pre_act * pre_act)
    tanh_val = jnp.tanh(inner)
    return 0.5 * (1.0 + tanh_val) + 0.5 * pre_act * (1.0 - tanh_val * tanh_val) * math.sqrt(
        2.0 / math.pi
    ) * (1.0 + 3.0 * 0.044715 * pre_act * pre_act)


def contract_last(left, right):
    return lax.dot_general(
        left, right, (((1,), (1,)), ((), ())), preferred_element_type=jnp.float32
    )


def contract_first(left, right):
    return lax.dot_general(
        left, right, (((0,), (0,)), ((), ())), preferred_element_type=jnp.float32
    )


def local(aggregated, cotangent, kernel_in, kernel_out, tile_values, tile_cols, tile_count):
    row_count = aggregated.shape[0]
    group_size = lax.axis_size("rep")
    norm_factor = 1.0 / math.sqrt(row_count * lax.axis_size("node") * group_size)
    agg_piece = lax.all_gather(aggregated, "rep", axis=0, tiled=True)
    cot_piece = lax.all_gather(cotangent, "rep", axis=0, tiled=True)
    pre_act = jnp.dot(agg_piece, kernel_in, preferred_element_type=jnp.float32)
    act_out = gelu_value(pre_act).astype(jnp.bfloat16)
    grad_act = contract_last(cot_piece, kernel_out)
    grad_pre = (grad_act * gelu_slope(pre_act)).astype(jnp.bfloat16)
    sum_out = contract_first(act_out, cot_piece)
    sum_in = contract_first(agg_piece, grad_pre)
    sum_in, sum_out, hidden_buf = (sum_in, sum_out, grad_pre)
    grad_agg = lax.psum_scatter(
        contract_last(hidden_buf, kernel_in).astype(jnp.bfloat16),
        "rep",
        scatter_dimension=0,
        tiled=True,
    )
    total_in, total_out = lax.psum((sum_in, sum_out), "node")
    grad_in = total_in * norm_factor
    grad_out = total_out * norm_factor
    tiles = tile_values[0]
    slot_cols = tile_cols[0]
    slot_ids = jnp.arange(tiles.shape[0], dtype=jnp.int32)
    live = slot_ids < tile_count[0]
    terms = jnp.einsum("trc,rd->tcd", tiles, grad_agg, preferred_element_type=jnp.float32)
    targets = jnp.arange(3, dtype=jnp.int32)
    select = ((slot_cols[None, :] == targets[:, None]) & live[None, :]).astype(jnp.float32)
    by_target = jnp.einsum("kt,tcd->kcd", select, terms)
    outgoing = jnp.concatenate([by_target[0], by_target[2]], axis=0)
    padded = with_halo(outgoing.astype(jnp.bfloat16), (("node", 0),), row_count).astype(
        outgoing.dtype
    )
    from_left = padded[:row_count]
    from_right = padded[3 * row_count :]
    grad_nodes = (cotangent.astype(jnp.float32) + by_target[1] + from_left + from_right).astype(
        jnp.bfloat16
    )
    return (grad_nodes, grad_in, grad_out)


def solution(mesh):
    return jax.shard_map(
        local,
        mesh=mesh,
        in_specs=(
            P(("node", "rep"), None),
            P(("node", "rep"), None),
            P(None, "rep"),
            P("rep", None),
            P(("node", "rep"), None, None, None),
            P(("node", "rep"), None),
            P(("node", "rep")),
        ),
        out_specs=(P(("node", "rep"), None), P(None, "rep"), P("rep", None)),
        check_vma=False,
    )
```

profile of v0, /device:TPU:1, one launch (start us, length us, event | category | flops | bytes accessed | tf_op | source)
XLA Modules:
  0.0 738.4 jit_solution(5127932269936591329)
XLA Ops:
  7.2 0.7 all-gather.5.cloned.1.call-update
  8.0 0.7 all-gather.3.cloned.1.call-update
  8.7 0.0 reduce-scatter.2.cloned.1.call-start
  8.7 112.6 %all-gather.5.cloned.1.call-done = bf16[4096,512]{1,0:T(8,128)(2,1)} async-done(((bf16[256,512]{1,0:T(8,128)(2,1)}), bf16[4096,512]{1,0:T(8,128)(2,1)}) %all-gather.5.cloned.1.call-update) | async-done | bytes 4194320 | tf_op jit(solution)/shard_map/all_gather | solution.py:52
  121.3 4.8 fusion.27
  126.1 102.4 %all-gather.3.cloned.1.call-done = bf16[4096,512]{1,0:T(8,128)(2,1)} async-done(((bf16[256,512]{1,0:T(8,128)(2,1)}), bf16[4096,512]{1,0:T(8,128)(2,1)}) %all-gather.3.cloned.1.call-update) | async-done | bytes 4194320 | tf_op jit(solution)/shard_map/all_gather | solution.py:53
  228.4 4.4 fusion
  232.9 3.2 convolution_convert_fusion
  236.1 0.0 all-reduce.3.cloned.1.call-start
  236.9 3.8 convolution_bitcast_fusion.1
  240.7 4.2 fusion.6
  244.9 95.9 %reduce-scatter.2.cloned.1.call-done = bf16[256,512]{1,0:T(8,128)(2,1)} async-done(((bf16[4096,512]{1,0:T(8,128)(2,1)}), bf16[256,512]{1,0:T(8,128)(2,1)}) %reduce-scatter.2.cloned.1.call-update) | async-done | bytes 262160 | tf_op jit(solution)/shard_map/reduce_scatter | solution.py:61
  340.8 1.4 convolution_bitcast_fusion
  342.2 1.0 copy.16
  343.3 2.1 fusion.26
  345.4 0.7 fusion.25
  346.2 4.6 collective-permute-start.1
  350.8 3.4 collective-permute-start
  354.2 371.1 %all-reduce.3.cloned.1.call-done = (f32[512,128]{0,1:T(8,128)}, f32[128,512]{1,0:T(8,128)}) async-done(((f32[512,128]{0,1:T(8,128)}, f32[128,512]{1,0:T(8,128)}), (f32[512,128]{0,1:T(8,128)}, f32[128,512]{1,0:T(8,128)})) %all-reduce.3.cloned.1.call-update) | async-done | bytes 524304 | tf_op jit(solution)/shard_map/psum | solution.py:67
  725.4 1.0 broadcast_multiply_fusion.1
  726.3 0.8 copy.17
  727.2 1.7 broadcast_multiply_fusion
  728.9 2.1 slice.24
  731.0 0.9 fusion.12
  (21 shorter events, 0.2 us)
Async XLA Ops:
  7.2 333.7 %copy-start = (bf16[1,4,256,256]{3,2,1,0:T(8,128)(2,1)S(1)}, bf16[1,4,256,256]{3,2,1,0:T(8,128)(2,1)}, u32[]{:S(2)}) copy-start(bf16[1,4,256,256]{3,2,1,0:T(8,128)(2,1)} %param.11) | copy-start | bytes 1572868
  7.2 114.1 %all-gather.5.cloned.1.call-start = ((), (), s32[]{:S(2)}) async-start(), calls=%async_computation.2 | async-start | bytes 4456448 | tf_op jit(solution)/shard_map/all_gather | solution.py:52
  7.9 220.5 %all-gather.3.cloned.1.call-start = ((), (), s32[]{:S(2)}) async-start(), calls=%async_computation.1 | async-start | bytes 4456448 | tf_op jit(solution)/shard_map/all_gather | solution.py:53
  8.7 219.8 %copy-start.5 = (bf16[128,512]{1,0:T(8,128)(2,1)S(1)}, bf16[128,512]{1,0:T(8,128)(2,1)}, u32[]{:S(2)}) copy-start(bf16[128,512]{1,0:T(8,128)(2,1)} %param.10) | copy-start | bytes 393220
  8.7 332.1 %reduce-scatter.2.cloned.1.call-start = ((), (), s32[]{:S(2)}) async-start(), calls=%async_computation.3 | async-start | bytes 4456448 | tf_op jit(solution)/shard_map/reduce_scatter | solution.py:61
  126.1 106.8 %copy-start.3 = (bf16[512,128]{1,0:T(8,128)(2,1)S(1)}, bf16[512,128]{1,0:T(8,128)(2,1)}, u32[]{:S(2)}) copy-start(bf16[512,128]{1,0:T(8,128)(2,1)} %param.9) | copy-start | bytes 393220
  236.1 489.2 %all-reduce.3.cloned.1.call-start = ((), (), s32[]{:S(2)}) async-start(), calls=%async_computation.4 | async-start | bytes 1048576 | tf_op jit(solution)/shard_map/psum | solution.py:67
  236.9 3.8 copy-start.1
  244.9 98.4 %copy-start.4 = (s32[1,4]{1,0:T(1,128)S(1)}, s32[1,4]{1,0:T(1,128)}, u32[]{:S(2)}) copy-start(s32[1,4]{1,0:T(1,128)} %param.12) | copy-start | bytes 52
  346.1 384.9 %copy-start.2 = (bf16[256,512]{1,0:T(8,128)(2,1)S(1)}, bf16[256,512]{1,0:T(8,128)(2,1)}, u32[]{:S(2)}) copy-start(bf16[256,512]{1,0:T(8,128)(2,1)} %param.8) | copy-start | bytes 786436
  346.2 384.8 %collective-permute-start.1 = (bf16[256,512]{1,0:T(8,128)(2,1)S(1)}, bf16[256,512]{1,0:T(8,128)(2,1)S(1)}, u32[]{:S(2)}, u32[]{:S(2)}) collective-permute-start(bf16[256,512]{1,0:T(8,128)(2,1)S(1)} %bitcast.40), channel_id=1, source_target_pairs={{16,0},{32,16},{48,32},{64,48},{80,64},{96,80},{112,96},{128,112},... | collective-permute-start | bytes 786440 | tf_op jit(solution)/shard_map/ppermute | solution.py:18
  350.8 380.2 %collective-permute-start = (bf16[256,512]{1,0:T(8,128)(2,1)S(1)}, bf16[256,512]{1,0:T(8,128)(2,1)S(1)}, u32[]{:S(2)}, u32[]{:S(2)}) collective-permute-start(bf16[256,512]{1,0:T(8,128)(2,1)S(1)} %bitcast.38), channel_id=1, source_target_pairs={{0,16},{16,32},{32,48},{48,64},{64,80},{80,96},{96,112},{112,128},... | collective-permute-start | bytes 786440 | tf_op jit(solution)/shard_map/ppermute | solution.py:15
Sparse Core Ops, SparseCore 0:
  10.4 110.8 all-gather.4
  123.6 104.7 all-gather.2
  236.3 104.5 reduce-scatter.1
  344.5 380.7 all-reduce.2
where the time goes:
time: 739 us; the launch traced here: 738 us
  waiting for transfers between devices  683 us (92%)
  matrix products  24 us (3%)
  between operations  14.6 us (2%)
  starting transfers between devices  8.16 us (1%)
    psum x1, waiting for transfers between devices, local(): total_in, total_out = lax.psum((sum_in, sum_out), 'node')  371 us
    all_gather x1, waiting for transfers between devices, local(): agg_piece = lax.all_gather(aggregated, 'rep', axis=0, tiled=True)  113 us
    all_gather x1, waiting for transfers between devices, local(): cot_piece = lax.all_gather(cotangent, 'rep', axis=0, tiled=True)  102 us
    reduce_scatter x1, waiting for transfers between devices, local(): lax.psum_scatter(contract_last(hidden_buf, kernel_in).astype(jnp.bfloat16...  95.9 us
  transfers between devices with their start and end apart: 6, of which 4 were waited for; matrix products, arithmetic and copies ran while one was open for 3% of the time, Pallas kernels for 0%

commit v1 on v0

v1 whole, which is shorter than its diff:
```python
import functools
import math

import jax
import jax.numpy as jnp
from jax import lax
from jax.experimental import pallas as pl
from jax.experimental.pallas import tpu as pltpu
from jax.sharding import PartitionSpec as P

MESH = pl.DeviceIdType.MESH
BF16 = jnp.bfloat16
F32 = jnp.float32
X_HI, X_LO, CORES, Z_LO = 2, 2, 2, 3
GELU_C = math.sqrt(2.0 / math.pi)


def dot(left, right):
    return jnp.dot(left, right, preferred_element_type=F32)


def dot_last(left, right):
    return lax.dot_general(left, right, (((1,), (1,)), ((), ())), preferred_element_type=F32)


def mirror(i, ny):
    if i == 0 or i == ny - 1:
        return i
    return i + 1 if i % 2 == 1 else i - 1


def kernel(
    dims,
    agg_ref, cot_ref, kin_ref, kout_ref, tiles_ref, cols_ref, count_ref,
    nodes_ref, grads_ref,
    rows_a, rows_c, at, ct, tiles_t, wts, part, from_core, chain, chain_out, acc, back_out, back_in,
    halo_out, halo_in, pieces, piece_in, triple, triple_in, total,
    s_ring, r_ring, s_core, r_core, s_x, r_x, s_part, r_part, s_chain, r_chain, s_back, r_back,
    s_halo, r_halo, s_piece, r_piece, s_tri, r_tri, s_tot, r_tot, s_swap, r_swap,
):
    ny, nz = dims
    zq_n = nz // Z_LO
    npiece = X_HI * zq_n
    nrow, feat = agg_ref.shape
    node, rep = lax.axis_index("node"), lax.axis_index("rep")
    core = lax.rem(node, CORES)
    z = lax.rem(lax.div(node, CORES), nz)
    xh = lax.div(node, CORES * nz)
    y, xl = lax.div(rep, X_LO), lax.rem(rep, X_LO)
    zq, zr = lax.div(z, Z_LO), lax.rem(z, Z_LO)
    other = 1 - core
    sign = 1 - 2 * core
    nodes = X_HI * nz * CORES

    def dev(xh, xl, y, z, core):
        return (xh * (nz * CORES) + z * CORES + core, y * X_LO + xl)

    mate = dev(xh, xl, y, z, other)
    across = dev(lax.rem(xh + core, X_HI), 1 - xl, y, z, core)
    y_fwd = dev(xh, xl, lax.rem(y + sign + ny, ny), z, core)
    y_bwd = dev(xh, xl, lax.rem(y - sign + ny, ny), z, core)
    nxt = (lax.rem(node + 1, nodes), rep)
    prv = (lax.rem(node + nodes - 1, nodes), rep)
    my_piece = xh * zq_n + zq
    scatter_peers = []
    for j in range(1, npiece):
        pxh = lax.rem(xh + j // zq_n, X_HI)
        pzq = lax.rem(zq + j % zq_n, zq_n)
        scatter_peers.append((j, dev(pxh, xl, y, pzq * Z_LO + zr, core), pxh * zq_n + pzq))
    tri_peers = []
    for j in range(1, Z_LO):
        tri_peers.append((j, dev(xh, xl, y, zq * Z_LO + lax.rem(zr + j, Z_LO), core)))

    barrier = pltpu.get_barrier_semaphore()
    peers = [mate, across, y_fwd, y_bwd, nxt, prv]
    peers += [d for _, d, _ in scatter_peers] + [d for _, d in tri_peers]
    for peer in peers:
        pl.semaphore_signal(barrier, inc=1, device_id=peer, device_id_type=MESH)

    own, far = pl.ds(0, nrow), pl.ds(nrow, nrow)
    wts[0, 0] = kin_ref[...]
    wts[1, 0] = kout_ref[...].T
    rows_a[own] = agg_ref[...]
    rows_c[own] = cot_ref[...]
    at[:, own] = agg_ref[...].T
    ct[:, own] = cot_ref[...].T
    for t in range(tiles_ref.shape[1]):
        tiles_t[t] = tiles_ref[0, t].T
    acc[...] = jnp.zeros_like(acc)
    pl.semaphore_wait(barrier, len(peers))

    started = []

    def send(src, dst, s_sem, r_sem, device):
        copy = pltpu.make_async_remote_copy(
            src_ref=src, dst_ref=dst, send_sem=s_sem, recv_sem=r_sem, device_id=device, device_id_type=MESH
        )
        copy.start()
        started.append(copy)

    def arrive(dst, s_sem, r_sem, device):
        pltpu.make_async_remote_copy(
            src_ref=dst, dst_ref=dst, send_sem=s_sem, recv_sem=r_sem, device_id=device, device_id_type=MESH
        ).wait_recv()

    send(wts.at[core, 0], wts.at[core, 1], s_ring.at[1], r_ring.at[1], y_fwd)
    send(wts.at[core, 0], wts.at[core, 2], s_ring.at[2], r_ring.at[2], y_bwd)
    send(agg_ref, rows_a.at[far], s_x.at[0], r_x.at[0], across)
    send(cot_ref, rows_c.at[far], s_x.at[1], r_x.at[1], across)

    def ring_step(i):
        arrive(wts.at[core, i], s_ring.at[i], r_ring.at[i], y_bwd if i % 2 == 1 else y_fwd)
        if i + 2 < ny:
            send(
                wts.at[core, i], wts.at[core, i + 2], s_ring.at[i + 2], r_ring.at[i + 2],
                y_fwd if i % 2 == 1 else y_bwd,
            )
        j = mirror(i, ny)
        send(wts.at[core, i], wts.at[core, j], s_core.at[i], r_core.at[j], mate)

    def process(i):
        if i > 0:
            arrive(wts.at[other, i], s_core.at[i], r_core.at[i], mate)
        pre = dot(rows_a[...], wts[0, i])
        g_act = dot(rows_c[...], wts[1, i])
        sq = pre * pre
        th = jnp.tanh(GELU_C * (pre + 0.044715 * sq * pre))
        half = 0.5 * (1.0 + th)
        act = (pre * half).astype(BF16)
        slope = half + 0.5 * pre * (1.0 - th * th) * GELU_C * (1.0 + 3.0 * 0.044715 * sq)
        g_pre = (g_act * slope).astype(BF16)
        part[1, i] = dot(ct[...], act).astype(BF16)
        part[0, i] = dot(at[...], g_pre).astype(BF16)
        send(part.at[other, i], from_core.at[mirror(i, ny)], s_part.at[i], r_part.at[mirror(i, ny)], mate)
        acc[...] += dot_last(g_pre, wts[0, i])

    def far_rows():
        arrive(rows_a.at[far], s_x.at[0], r_x.at[0], across)
        arrive(rows_c.at[far], s_x.at[1], r_x.at[1], across)
        at[:, far] = rows_a[far].T
        ct[:, far] = rows_c[far].T

    todo = 0
    for i in range(1, ny):
        ring_step(i)
        if i == 2:
            far_rows()
            process(0)
            todo = 1
        elif i >= 4 and i % 2 == 0:
            process(todo)
            process(todo + 1)
            todo += 2
    for i in range(todo, ny):
        process(i)

    back_out[...] = acc[far].astype(BF16)
    send(back_out, back_in, s_back, r_back, across)

    def chain_step(i):
        arrive(from_core.at[i], s_part.at[i], r_part.at[i], mate)
        tot = part[core, i].astype(F32) + from_core[i].astype(F32)
        if i == 0:
            feeds = [1, 2]
        else:
            feeds = [i + 2] if i + 2 < ny else []
        for f in feeds:
            arrive(chain.at[f], s_chain.at[f], r_chain.at[f], y_fwd if f % 2 == 1 else y_bwd)
            tot = tot + chain[f].astype(F32)
        if i == 0:
            return tot
        chain_out[i] = tot.astype(BF16)
        send(chain_out.at[i], chain.at[i], s_chain.at[i], r_chain.at[i], y_bwd if i % 2 == 1 else y_fwd)

    chain_step(ny - 1)
    chain_step(ny - 2)

    arrive(back_in, s_back, r_back, across)
    g_agg = (acc[own] + back_in[...].astype(F32)).astype(BF16)
    live_count = count_ref[0]
    sums = [None, None, None]
    for t in range(tiles_ref.shape[1]):
        term = dot(tiles_t[t], g_agg)
        for k in range(3):
            on = jnp.logical_and(cols_ref[0, t] == k, t < live_count)
            add = term * jnp.where(on, 1.0, 0.0).astype(F32)
            sums[k] = add if sums[k] is None else sums[k] + add
    halo_out[0] = sums[0].astype(BF16)
    halo_out[1] = sums[2].astype(BF16)
    acc[own] = sums[1] + cot_ref[...].astype(F32)
    send(halo_out.at[0], halo_in.at[0], s_halo.at[0], r_halo.at[0], prv)
    send(halo_out.at[1], halo_in.at[1], s_halo.at[1], r_halo.at[1], nxt)

    for i in range(ny - 3, 0, -1):
        chain_step(i)
    mine = chain_step(0)

    prow = feat // npiece
    for p in range(npiece):
        pieces[p] = mine[p * prow : (p + 1) * prow].astype(BF16)
    for j, peer, p in scatter_peers:
        send(pieces.at[p], piece_in.at[j], s_piece.at[j], r_piece.at[j], peer)

    arrive(halo_in.at[0], s_halo.at[0], r_halo.at[0], nxt)
    arrive(halo_in.at[1], s_halo.at[1], r_halo.at[1], prv)
    nodes_ref[...] = (acc[own] + halo_in[1].astype(F32) + halo_in[0].astype(F32)).astype(BF16)

    tot = pieces[my_piece].astype(F32)
    for j, peer, _ in scatter_peers:
        arrive(piece_in.at[j], s_piece.at[j], r_piece.at[j], peer)
        tot = tot + piece_in[j].astype(F32)
    triple[...] = tot.astype(BF16)
    for j, peer in tri_peers:
        send(triple, triple_in.at[zr], s_tri.at[j], r_tri.at[j], peer)
    triple_in[zr] = triple[...]
    for j, peer in tri_peers:
        arrive(triple_in.at[lax.rem(zr + Z_LO - j, Z_LO)], s_tri.at[j], r_tri.at[j], peer)
    tot = triple_in[0].astype(F32)
    for k in range(1, Z_LO):
        tot = tot + triple_in[k].astype(F32)
    total[core, my_piece] = tot.astype(BF16)
    for j, peer, _ in scatter_peers:
        send(total.at[core, my_piece], total.at[core, my_piece], s_tot.at[j], r_tot.at[j], peer)
    for j, peer, _ in scatter_peers:
        fxh = lax.rem(xh + X_HI - j // zq_n, X_HI)
        fzq = lax.rem(zq + zq_n - j % zq_n, zq_n)
        arrive(total.at[core, fxh * zq_n + fzq], s_tot.at[j], r_tot.at[j], peer)
    send(total.at[core], total.at[core], s_swap, r_swap, mate)
    arrive(total.at[other], s_swap, r_swap, mate)
    for m in range(2):
        for p in range(npiece):
            grads_ref[m, p * prow : (p + 1) * prow, :] = total[m, p]
    for copy in started:
        copy.wait_send()


def local(nz, aggregated, cotangent, kernel_in, kernel_out, tile_values, tile_cols, tile_count):
    nrow, feat = aggregated.shape
    ny = lax.axis_size("rep") // X_LO
    hid = kernel_in.shape[1]
    slots = tile_values.shape[1]
    npiece = X_HI * (nz // Z_LO)
    norm_factor = 1.0 / math.sqrt(nrow * lax.axis_size("node") * lax.axis_size("rep"))
    vmem = lambda shape, dtype=BF16: pltpu.VMEM(shape, dtype)
    dma = lambda *shape: pltpu.SemaphoreType.DMA(shape)
    full = pl.BlockSpec(memory_space=pltpu.VMEM)
    scalars = pl.BlockSpec(memory_space=pltpu.SMEM)
    grad_nodes, grads = pl.pallas_call(
        functools.partial(kernel, (ny, nz)),
        out_shape=(
            jax.ShapeDtypeStruct((nrow, feat), BF16),
            jax.ShapeDtypeStruct((2, feat, hid), BF16),
        ),
        in_specs=[full] * 5 + [scalars] * 2,
        out_specs=(full, full),
        scratch_shapes=[
            vmem((2 * nrow, feat)),
            vmem((2 * nrow, feat)),
            vmem((feat, 2 * nrow)),
            vmem((feat, 2 * nrow)),
            vmem((slots, nrow, nrow)),
            vmem((2, ny, feat, hid)),
            vmem((2, ny, feat, hid)),
            vmem((ny, feat, hid)),
            vmem((ny, feat, hid)),
            vmem((ny, feat, hid)),
            vmem((2 * nrow, feat), F32),
            vmem((nrow, feat)),
            vmem((nrow, feat)),
            vmem((2, nrow, feat)),
            vmem((2, nrow, feat)),
            vmem((npiece, feat // npiece, hid)),
            vmem((npiece, feat // npiece, hid)),
            vmem((feat // npiece, hid)),
            vmem((Z_LO, feat // npiece, hid)),
            vmem((2, npiece, feat // npiece, hid)),
            dma(ny), dma(ny),
            dma(ny), dma(ny),
            dma(2), dma(2),
            dma(ny), dma(ny),
            dma(ny), dma(ny),
            pltpu.SemaphoreType.DMA, pltpu.SemaphoreType.DMA,
            dma(2), dma(2),
            dma(npiece), dma(npiece),
            dma(Z_LO), dma(Z_LO),
            dma(npiece), dma(npiece),
            pltpu.SemaphoreType.DMA, pltpu.SemaphoreType.DMA,
        ],
        compiler_params=pltpu.CompilerParams(
            collective_id=0, has_side_effects=True, vmem_limit_bytes=48 << 20
        ),
    )(aggregated, cotangent, kernel_in, kernel_out, tile_values, tile_cols, tile_count)
    grad_in = grads[0].astype(F32) * norm_factor
    grad_out = grads[1].T.astype(F32) * norm_factor
    return (grad_nodes, grad_in, grad_out)


def solution(mesh):
    nz = mesh.shape["node"] // (X_HI * CORES)
    return jax.shard_map(
        functools.partial(local, nz),
        mesh=mesh,
        in_specs=(
            P(("node", "rep"), None),
            P(("node", "rep"), None),
            P(None, "rep"),
            P("rep", None),
            P(("node", "rep"), None, None, None),
            P(("node", "rep"), None),
            P(("node", "rep")),
        ),
        out_specs=(P(("node", "rep"), None), P(None, "rep"), P("rep", None)),
        check_vma=False,
    )
```

time: 739 us -> 91.7 us (0.12)
  waiting for transfers between devices: 683 us -> 0 us
  Pallas kernels: 0 us -> 82.1 us
  matrix products: 24 us -> 0 us
  between operations: 14.6 us -> 1.33 us
  starting transfers between devices: 8.16 us -> 0 us
    psum x1 -> x0, waiting for transfers between devices: 371 us -> none  [local(): total_in, total_out = lax.psum((sum_in, sum_out), 'node')]
    all_gather x2 -> x0, waiting for transfers between devices: 215 us -> none  [the longest x1 113 us: local(): agg_piece = lax.all_gather(aggregated, 'rep', axis=0, tiled=True)]
    reduce_scatter x1 -> x0, waiting for transfers between devices: 95.9 us -> none  [local(): lax.psum_scatter(contract_last(hidden_buf, kernel_in).astype(jnp.bfloat16...]
    pallas_call x0 -> x1, Pallas kernels: none -> 82.1 us  [local(): pl.pallas_call(functools.partial(kernel, (ny, nz)), out_shape=(jax.ShapeD...]
    dot_general x7 -> x0, matrix products: 24 us -> none  [the longest x2 8.01 us: contract_first(): lax.dot_general(left, right, (((0,), (0,)), ((), ())), preferred_element_...]
    ppermute x2 -> x0, starting transfers between devices: 8.01 us -> none  [the longest x1 4.6 us: with_halo(): lax.ppermute(lax.slice_in_dim(block, 0, width, axis=dim), axis, backward)]
  transfers between devices with their start and end apart: 6 -> 0, of which waited for: 4 -> 0; matrix products, arithmetic and copies ran while one was open for 3% -> 0% of each run, Pallas kernels for 0% -> 0%
where the time goes in v1:
time: 91.7 us; the launch traced here: 90.5 us
  Pallas kernels  82.1 us (90%)
  local copies, waits for them, and re-layouts  6.28 us (7%)
  between operations  1.33 us (1%)
    pallas_call x1, Pallas kernels, local(): pl.pallas_call(functools.partial(kernel, (ny, nz)), out_shape=(jax.ShapeD...  82.1 us
    unnamed x14, local copies, waits for them, and re-layouts  6.28 us

profile of v1, /device:TPU:1, one launch (start us, length us, event | category | flops | bytes accessed | tf_op | source)
XLA Modules:
  0.0 90.5 jit_solution(17778543490110785482)
XLA Ops:
  0.6 0.0 copy-start.5
  1.3 0.0 copy-done.5
  1.3 0.0 copy-start
  1.3 1.0 %copy-done = bf16[1,4,256,256]{3,2,1,0:T(8,128)(2,1)S(1)} copy-done((bf16[1,4,256,256]{3,2,1,0:T(8,128)(2,1)S(1)}, bf16[1,4,256,256]{3,2,1,0:T(8,128)(2,1)}, u32[]{:S(2)}) %copy-start) | copy-done | bytes 524312
  2.4 0.0 copy-start.1
  2.4 0.9 %copy-done.1 = bf16[256,512]{1,0:T(8,128)(2,1)S(1)} copy-done((bf16[256,512]{1,0:T(8,128)(2,1)S(1)}, bf16[256,512]{1,0:T(8,128)(2,1)}, u32[]{:S(2)}) %copy-start.1) | copy-done | bytes 262168
  3.3 0.0 copy-start.2
  3.3 0.9 %copy-done.2 = bf16[256,512]{1,0:T(8,128)(2,1)S(1)} copy-done((bf16[256,512]{1,0:T(8,128)(2,1)S(1)}, bf16[256,512]{1,0:T(8,128)(2,1)}, u32[]{:S(2)}) %copy-start.2) | copy-done | bytes 262168
  4.3 0.0 copy-start.3
  4.3 0.9 copy-done.3
  5.2 0.0 copy-start.4
  5.2 0.9 copy-done.4
  6.1 82.1 %shard_map.94 = (bf16[256,512]{1,0:T(8,128)(2,1)S(1)}, bf16[2,512,128]{2,1,0:T(8,128)(2,1)S(1)}) custom-call(bf16[256,512]{1,0:T(8,128)(2,1)S(1)} %copy-done.1, bf16[256,512]{1,0:T(8,128)(2,1)S(1)} %copy-done.2, bf16[512,128]{1,0:T(8,128)(2,1)S(1)} %copy-done.3, bf16[128,512]{1,0:T(8,128)(2,1)S(1)} %copy-done.4, bf16[1,4,256,256]{3,2,1,0:T(8,128)(2,1)S(1)} %copy-done, ...), custom_call_target="tpu_custom_call" | custom-call | tf_op jit(solution)/shard_map/pallas_call | solution.py:248
  88.2 0.7 multiply_bitcast_fusion
  88.9 0.8 copy.10
  89.8 0.7 copy.13
Async XLA Ops:
  0.6 0.7 copy-start.5
  1.3 1.0 %copy-start = (bf16[1,4,256,256]{3,2,1,0:T(8,128)(2,1)S(1)}, bf16[1,4,256,256]{3,2,1,0:T(8,128)(2,1)}, u32[]{:S(2)}) copy-start(bf16[1,4,256,256]{3,2,1,0:T(8,128)(2,1)} %tiles_ref.1) | copy-start | bytes 1572868
  2.4 0.9 %copy-start.1 = (bf16[256,512]{1,0:T(8,128)(2,1)S(1)}, bf16[256,512]{1,0:T(8,128)(2,1)}, u32[]{:S(2)}) copy-start(bf16[256,512]{1,0:T(8,128)(2,1)} %agg_ref.1) | copy-start | bytes 786436
  3.3 0.9 %copy-start.2 = (bf16[256,512]{1,0:T(8,128)(2,1)S(1)}, bf16[256,512]{1,0:T(8,128)(2,1)}, u32[]{:S(2)}) copy-start(bf16[256,512]{1,0:T(8,128)(2,1)} %cot_ref.1) | copy-start | bytes 786436
  4.3 0.9 copy-start.3
  5.2 0.9 copy-start.4

commit v2 on v0

v2 whole, which is shorter than its diff:
```python
import functools
import math

import jax
import jax.numpy as jnp
from jax import lax
from jax.experimental import pallas as pl
from jax.experimental.pallas import tpu as pltpu
from jax.sharding import PartitionSpec as P

MESH = pl.DeviceIdType.MESH
BF16 = jnp.bfloat16
F32 = jnp.float32
X_HI, X_LO, CORES, NY, Z_IN = 2, 2, 2, 8, 4
HALF = NY // 2
GELU_C = math.sqrt(2.0 / math.pi)
N_SEM = 64


def dot(left, right):
    return jnp.dot(left, right, preferred_element_type=F32)


def dot_last(left, right):
    return lax.dot_general(left, right, (((1,), (1,)), ((), ())), preferred_element_type=F32)


def gelu_pair(pre, g_act):
    sq = pre * pre
    th = jnp.tanh(GELU_C * (pre + 0.044715 * sq * pre))
    half = 0.5 * (1.0 + th)
    slope = half + 0.5 * pre * (1.0 - th * th) * GELU_C * (1.0 + 3.0 * 0.044715 * sq)
    return (pre * half).astype(BF16), (g_act * slope).astype(BF16)


def kernel(
    nz,
    agg_ref, cot_ref, kin_ref, kout_ref, tiles_ref, cols_ref, count_ref,
    nodes_ref, gin_ref, gout_ref,
    rows_a, rows_c, at, ct, tiles, w_in, w_out, act, gpre, part, first, first_out, mid_in, fin_in,
    acc, back_out, back_in, halo_out, halo_in, pieces, piece_in, triple, triple_in, total,
    s_sem, r_sem, l_sem,
):
    zg_n = nz // Z_IN
    npiece = X_HI * Z_IN
    nrow, feat = agg_ref.shape
    node, rep = lax.axis_index("node"), lax.axis_index("rep")
    core = lax.rem(node, CORES)
    z = lax.rem(lax.div(node, CORES), nz)
    xh = lax.div(node, CORES * nz)
    y, xl = lax.div(rep, X_LO), lax.rem(rep, X_LO)
    zg, zi = lax.div(z, Z_IN), lax.rem(z, Z_IN)
    other = 1 - core
    sign = 1 - 2 * core
    nodes = X_HI * nz * CORES

    def dev(xh, xl, y, z, core):
        return (xh * (nz * CORES) + z * CORES + core, y * X_LO + xl)

    def along_y(step, on_core):
        return dev(xh, xl, lax.rem(y + step + NY, NY), z, on_core)

    mate = dev(xh, xl, y, z, other)
    across = dev(lax.rem(xh + core, X_HI), 1 - xl, y, z, core)
    y_fwd, y_bwd, y_bwd2 = along_y(sign, core), along_y(-sign, core), along_y(-2 * sign, core)
    nxt = (lax.rem(node + 1, nodes), rep)
    prv = (lax.rem(node + nodes - 1, nodes), rep)
    my_piece = xh * Z_IN + zi
    scatter_peers = []
    for j in range(1, npiece):
        pxh = lax.rem(xh + j // Z_IN, X_HI)
        pzi = lax.rem(zi + j % Z_IN, Z_IN)
        scatter_peers.append((j, dev(pxh, xl, y, zg * Z_IN + pzi, core), pxh * Z_IN + pzi))
    tri_peers = []
    for j in range(1, zg_n):
        tri_peers.append((j, dev(xh, xl, y, lax.rem(zg + j, zg_n) * Z_IN + zi, core)))

    barrier = pltpu.get_barrier_semaphore()
    peers = [mate, across, y_fwd, y_bwd, along_y(sign, other), along_y(-sign, other)]
    peers += [along_y(2, core), along_y(-2, core), along_y(HALF, core), along_y(HALF, other), nxt, prv]
    peers += [d for _, d, _ in scatter_peers] + [d for _, d in tri_peers]
    for peer in peers:
        pl.semaphore_signal(barrier, inc=1, device_id=peer, device_id_type=MESH)

    own, by_mate, by_x, by_x_mate = [pl.ds(k * nrow, nrow) for k in range(4)]
    near, far = pl.ds(0, 2 * nrow), pl.ds(2 * nrow, 2 * nrow)
    loads = [
        pltpu.make_async_copy(agg_ref, rows_a.at[own], l_sem.at[0]),
        pltpu.make_async_copy(cot_ref, rows_c.at[own], l_sem.at[1]),
        pltpu.make_async_copy(tiles_ref.at[0], tiles, l_sem.at[2]),
    ]
    shard_loads = [
        pltpu.make_async_copy(kin_ref, w_in.at[0], l_sem.at[3]),
        pltpu.make_async_copy(kout_ref, w_out.at[0], l_sem.at[4]),
    ]
    for load in loads:
        load.start()

    @pl.when(core == 0)
    def _():
        for load in shard_loads:
            load.start()

    pl.semaphore_wait(barrier, len(peers))

    started = []
    used = [0]

    def ids(count=1):
        used[0] += count
        return used[0] - count

    def copy_to(src, dst, k, device, k_recv=None):
        return pltpu.make_async_remote_copy(
            src_ref=src, dst_ref=dst, send_sem=s_sem.at[k], recv_sem=r_sem.at[k if k_recv is None else k_recv],
            device_id=device, device_id_type=MESH,
        )

    def send(src, dst, k, device, k_recv=None):
        copy = copy_to(src, dst, k, device, k_recv)
        copy.start()
        started.append(copy)

    def arrive(dst, k):
        copy_to(dst, dst, k, mate).wait_recv()

    k_win, k_wout = ids(HALF), ids(HALF)
    k_anti_in, k_anti_out = ids(), ids()
    k_mate_rows, k_x_rows, k_fwd_rows = ids(2), ids(2), ids(2)
    k_mid = ids(4)
    k_fin, k_fin_anti, k_fin_mate = ids(4), ids(2), ids()
    k_back = ids(3)
    k_halo = ids(2)
    k_piece, k_tri, k_tot, k_swap = ids(npiece), ids(zg_n), ids(npiece), ids()
    assert used[0] <= N_SEM

    send(kin_ref, w_in.at[1], k_win + 1, y_fwd)
    send(kout_ref, w_out.at[1], k_wout + 1, y_fwd)
    send(agg_ref, rows_a.at[by_x], k_x_rows, across)
    send(cot_ref, rows_c.at[by_x], k_x_rows + 1, across)
    send(agg_ref, rows_a.at[by_mate], k_mate_rows, mate)
    send(cot_ref, rows_c.at[by_mate], k_mate_rows + 1, mate)
    opposite = along_y(HALF, core)
    anti_in = copy_to(kin_ref, w_in.at[0], k_anti_in, opposite)
    anti_out = copy_to(kout_ref, w_out.at[0], k_anti_out, opposite)

    @pl.when(core == 1)
    def _():
        anti_in.start()
        anti_out.start()

    acc[...] = jnp.zeros_like(acc)
    for load in loads:
        load.wait()

    def flip(block):
        at[:, block] = rows_a[block].T
        ct[:, block] = rows_c[block].T

    flip(own)
    arrive(rows_a.at[by_mate], k_mate_rows)
    arrive(rows_c.at[by_mate], k_mate_rows + 1)
    flip(by_mate)
    for t in range(tiles.shape[0]):
        tiles[t] = tiles[t].T

    def pass_on(j, last):
        for buf, k in ((w_in, k_win), (w_out, k_wout)):
            arrive(buf.at[j], k + j)
            if not last:
                send(buf.at[j], buf.at[j + 1], k + j + 1, y_fwd)

    def unit(j, rows):
        a, g = gelu_pair(dot(rows_a[rows], w_in[j]), dot_last(rows_c[rows], w_out[j]))
        act[j, rows] = a
        gpre[j, rows] = g

    def add_agg(j, rows):
        acc[rows] += dot_last(gpre[j, rows], w_in[j])

    def weight_terms(j):
        return dot(at[...], gpre[j]), dot(ct[...], act[j])

    pass_on(1, False)
    unit(1, near)
    add_agg(1, near)
    arrive(rows_a.at[by_x], k_x_rows)
    send(rows_a.at[by_x], rows_a.at[by_x_mate], k_fwd_rows, mate)
    pass_on(2, False)
    arrive(rows_c.at[by_x], k_x_rows + 1)
    send(rows_c.at[by_x], rows_c.at[by_x_mate], k_fwd_rows + 1, mate)
    flip(by_x)
    unit(2, near)
    add_agg(2, near)
    arrive(rows_a.at[by_x_mate], k_fwd_rows)
    arrive(rows_c.at[by_x_mate], k_fwd_rows + 1)
    flip(by_x_mate)
    unit(2, far)
    terms = weight_terms(2)
    for m in range(2):
        part[2, m] = terms[m].astype(BF16)
        send(part.at[2, m], mid_in.at[0, m], k_mid + m, y_bwd)
    add_agg(2, far)
    unit(1, far)
    terms = weight_terms(1)
    for m in range(2):
        first[m] = terms[m]
    add_agg(1, far)

    @pl.when(core == 0)
    def _():
        for load in shard_loads:
            load.wait()

    @pl.when(core == 1)
    def _():
        arrive(w_in.at[0], k_anti_in)
        arrive(w_out.at[0], k_anti_out)

    unit(0, near)
    unit(0, far)
    terms = weight_terms(0)
    for m in range(2):
        part[0, m] = terms[m].astype(BF16)
    own_to_mate = copy_to(part.at[0, 1], fin_in.at[3], k_fin_mate, mate)
    to_opposite = [
        copy_to(part.at[0, m], fin_in.at[2], k_fin_anti + m, along_y(HALF, m), k_fin_anti) for m in range(2)
    ]

    @pl.when(core == 0)
    def _():
        own_to_mate.start()
        fin_in[3] = part[0, 0]

    @pl.when(core == 1)
    def _():
        for copy in to_opposite:
            copy.start()

    add_agg(0, near)
    add_agg(0, far)
    pass_on(3, True)
    unit(3, near)
    unit(3, far)
    terms = weight_terms(3)
    for m in range(2):
        part[3, m] = terms[m].astype(BF16)
        send(part.at[3, m], mid_in.at[1, m], k_mid + 2 + m, y_bwd2)
    add_agg(3, near)
    add_agg(3, far)

    back_out[0] = acc[by_mate].astype(BF16)
    back_out[1] = acc[by_x_mate].astype(BF16)
    send(back_out.at[0], back_in.at[0], k_back, mate)
    send(back_out.at[1], back_in.at[1], k_back + 1, mate)

    for m in range(2):
        arrive(mid_in.at[0, m], k_mid + m)
        arrive(mid_in.at[1, m], k_mid + 2 + m)
        first_out[m] = (first[m] + mid_in[0, m].astype(F32) + mid_in[1, m].astype(F32)).astype(BF16)
        send(first_out.at[m], fin_in.at[core], k_fin + 2 * m, along_y(-sign, m), k_fin + core)

    arrive(back_in.at[1], k_back + 1)
    back_out[2] = (acc[by_x] + back_in[1].astype(F32)).astype(BF16)
    send(back_out.at[2], back_in.at[2], k_back + 2, across)

    arrive(fin_in.at[2], k_fin_anti)

    @pl.when(core == 1)
    def _():
        arrive(fin_in.at[3], k_fin_mate)

    mine = fin_in[3].astype(F32) + fin_in[2].astype(F32)
    for c in range(2):
        arrive(fin_in.at[c], k_fin + c)
        mine = mine + fin_in[c].astype(F32)

    prow = feat // npiece
    for p in range(npiece):
        pieces[p] = mine[p * prow : (p + 1) * prow].astype(BF16)
    for j, peer, p in scatter_peers:
        send(pieces.at[p], piece_in.at[j], k_piece + j, peer)

    arrive(back_in.at[0], k_back)
    arrive(back_in.at[2], k_back + 2)
    g_agg = (acc[own] + back_in[0].astype(F32) + back_in[2].astype(F32)).astype(BF16)
    live_count = count_ref[0]
    sums = [None, None, None]
    for t in range(tiles.shape[0]):
        term = dot(tiles[t], g_agg)
        for k in range(3):
            on = jnp.logical_and(cols_ref[0, t] == k, t < live_count)
            add = term * jnp.where(on, 1.0, 0.0).astype(F32)
            sums[k] = add if sums[k] is None else sums[k] + add
    halo_out[0] = sums[0].astype(BF16)
    halo_out[1] = sums[2].astype(BF16)
    acc[own] = sums[1] + rows_c[own].astype(F32)
    send(halo_out.at[0], halo_in.at[0], k_halo, prv)
    send(halo_out.at[1], halo_in.at[1], k_halo + 1, nxt)

    tot = pieces[my_piece].astype(F32)
    for j, peer, _ in scatter_peers:
        arrive(piece_in.at[j], k_piece + j)
        tot = tot + piece_in[j].astype(F32)
    triple[...] = tot.astype(BF16)
    for j, peer in tri_peers:
        send(triple, triple_in.at[zg], k_tri + j, peer)
    triple_in[zg] = triple[...]

    arrive(halo_in.at[0], k_halo)
    arrive(halo_in.at[1], k_halo + 1)
    nodes_ref[...] = (acc[own] + halo_in[1].astype(F32) + halo_in[0].astype(F32)).astype(BF16)

    for j, peer in tri_peers:
        arrive(triple_in.at[lax.rem(zg + zg_n - j, zg_n)], k_tri + j)
    tot = triple_in[0].astype(F32)
    for k in range(1, zg_n):
        tot = tot + triple_in[k].astype(F32)
    total[core, my_piece] = tot.astype(BF16)
    for j, peer, _ in scatter_peers:
        send(total.at[core, my_piece], total.at[core, my_piece], k_tot + j, peer)
    for j, peer, _ in scatter_peers:
        fxh = lax.rem(xh + X_HI - j // Z_IN, X_HI)
        fzi = lax.rem(zi + Z_IN - j % Z_IN, Z_IN)
        arrive(total.at[core, fxh * Z_IN + fzi], k_tot + j)
    send(total.at[core], total.at[core], k_swap, mate)
    arrive(total.at[other], k_swap)
    for p in range(npiece):
        gin_ref[p * prow : (p + 1) * prow, :] = total[0, p]
    gout_ref[...] = jnp.concatenate([total[1, p] for p in range(npiece)], axis=0).T
    for copy in started:
        copy.wait_send()

    @pl.when(core == 0)
    def _():
        own_to_mate.wait_send()

    @pl.when(core == 1)
    def _():
        anti_in.wait_send()
        anti_out.wait_send()
        for copy in to_opposite:
            copy.wait_send()


def local(nz, aggregated, cotangent, kernel_in, kernel_out, tile_values, tile_cols, tile_count):
    nrow, feat = aggregated.shape
    assert lax.axis_size("rep") == NY * X_LO
    hid = kernel_in.shape[1]
    slots = tile_values.shape[1]
    npiece = X_HI * Z_IN
    zg_n = nz // Z_IN
    prow = feat // npiece
    norm_factor = 1.0 / math.sqrt(nrow * lax.axis_size("node") * lax.axis_size("rep"))
    vmem = lambda shape, dtype=BF16: pltpu.VMEM(shape, dtype)
    full = pl.BlockSpec(memory_space=pltpu.VMEM)
    hbm = pl.BlockSpec(memory_space=pltpu.HBM)
    scalars = pl.BlockSpec(memory_space=pltpu.SMEM)
    grad_nodes, g_in, g_out = pl.pallas_call(
        functools.partial(kernel, nz),
        out_shape=(
            jax.ShapeDtypeStruct((nrow, feat), BF16),
            jax.ShapeDtypeStruct((feat, hid), BF16),
            jax.ShapeDtypeStruct((hid, feat), BF16),
        ),
        in_specs=[hbm] * 5 + [scalars] * 2,
        out_specs=(full, full, full),
        scratch_shapes=[
            vmem((4 * nrow, feat)),
            vmem((4 * nrow, feat)),
            vmem((feat, 4 * nrow)),
            vmem((feat, 4 * nrow)),
            vmem((slots, nrow, nrow)),
            vmem((HALF, feat, hid)),
            vmem((HALF, hid, feat)),
            vmem((HALF, 4 * nrow, hid)),
            vmem((HALF, 4 * nrow, hid)),
            vmem((HALF, 2, feat, hid)),
            vmem((2, feat, hid), F32),
            vmem((2, feat, hid)),
            vmem((2, 2, feat, hid)),
            vmem((4, feat, hid)),
            vmem((4 * nrow, feat), F32),
            vmem((3, nrow, feat)),
            vmem((3, nrow, feat)),
            vmem((2, nrow, feat)),
            vmem((2, nrow, feat)),
            vmem((npiece, prow, hid)),
            vmem((npiece, prow, hid)),
            vmem((prow, hid)),
            vmem((zg_n, prow, hid)),
            vmem((2, npiece, prow, hid)),
            pltpu.SemaphoreType.DMA((N_SEM,)),
            pltpu.SemaphoreType.DMA((N_SEM,)),
            pltpu.SemaphoreType.DMA((5,)),
        ],
        compiler_params=pltpu.CompilerParams(
            collective_id=0, has_side_effects=True, vmem_limit_bytes=62 << 20
        ),
    )(aggregated, cotangent, kernel_in, kernel_out, tile_values, tile_cols, tile_count)
    return (grad_nodes, g_in.astype(F32) * norm_factor, g_out.astype(F32) * norm_factor)


def solution(mesh):
    nz = mesh.shape["node"] // (X_HI * CORES)
    return jax.shard_map(
        functools.partial(local, nz),
        mesh=mesh,
        in_specs=(
            P(("node", "rep"), None),
            P(("node", "rep"), None),
            P(None, "rep"),
            P("rep", None),
            P(("node", "rep"), None, None, None),
            P(("node", "rep"), None),
            P(("node", "rep")),
        ),
        out_specs=(P(("node", "rep"), None), P(None, "rep"), P("rep", None)),
        check_vma=False,
    )
```

time: 739 us -> 82.6 us (0.11)
  waiting for transfers between devices: 683 us -> 0 us
  Pallas kernels: 0 us -> 77.7 us
  matrix products: 24 us -> 0 us
  between operations: 14.6 us -> 1.3 us
  starting transfers between devices: 8.16 us -> 0 us
    psum x1 -> x0, waiting for transfers between devices: 371 us -> none  [local(): total_in, total_out = lax.psum((sum_in, sum_out), 'node')]
    all_gather x2 -> x0, waiting for transfers between devices: 215 us -> none  [the longest x1 113 us: local(): agg_piece = lax.all_gather(aggregated, 'rep', axis=0, tiled=True)]
    reduce_scatter x1 -> x0, waiting for transfers between devices: 95.9 us -> none  [local(): lax.psum_scatter(contract_last(hidden_buf, kernel_in).astype(jnp.bfloat16...]
    pallas_call x0 -> x1, Pallas kernels: none -> 77.7 us  [local(): pl.pallas_call(functools.partial(kernel, nz), out_shape=(jax.ShapeDtypeSt...]
    dot_general x7 -> x0, matrix products: 24 us -> none  [the longest x2 8.01 us: contract_first(): lax.dot_general(left, right, (((0,), (0,)), ((), ())), preferred_element_...]
    ppermute x2 -> x0, starting transfers between devices: 8.01 us -> none  [the longest x1 4.6 us: with_halo(): lax.ppermute(lax.slice_in_dim(block, 0, width, axis=dim), axis, backward)]
  transfers between devices with their start and end apart: 6 -> 0, of which waited for: 4 -> 0; matrix products, arithmetic and copies ran while one was open for 3% -> 0% of each run, Pallas kernels for 0% -> 0%
where the time goes in v2:
time: 82.6 us; the launch traced here: 82.4 us
  Pallas kernels  77.7 us (94%)
  other arithmetic  2.4 us (3%)
  between operations  1.3 us (2%)
  local copies, waits for them, and re-layouts  0.99 us (1%)
    pallas_call x1, Pallas kernels, local(): pl.pallas_call(functools.partial(kernel, nz), out_shape=(jax.ShapeDtypeSt...  77.7 us
    mul x1, other arithmetic, local(): g_in.astype(F32) * norm_factor  1.66 us

profile of v2, /device:TPU:1, one launch (start us, length us, event | category | flops | bytes accessed | tf_op | source)
XLA Modules:
  0.0 82.4 jit_solution(9984316911382746641)
XLA Ops:
  1.3 77.7 %shard_map.94 = (bf16[256,512]{1,0:T(8,128)(2,1)}, bf16[512,128]{1,0:T(8,128)(2,1)}, bf16[128,512]{1,0:T(8,128)(2,1)}) custom-call(bf16[256,512]{1,0:T(8,128)(2,1)} %agg_ref.1, bf16[256,512]{1,0:T(8,128)(2,1)} %cot_ref.1, bf16[512,128]{1,0:T(8,128)(2,1)} %kin_ref.1, bf16[128,512]{1,0:T(8,128)(2,1)} %kout_ref.1, bf16[1,4,256,256]{3,2,1,0:T(8,128)(2,1)} %tiles_ref.1, ...), custom_call_target="tpu_custom_call" | custom-call | tf_op jit(solution)/shard_map/pallas_call | solution.py:359
  79.0 0.0 copy-start.1
  79.0 1.7 %convert_multiply_fusion.1 = f32[512,128]{1,0:T(8,128)} fusion(bf16[512,128]{1,0:T(8,128)(2,1)} %get-tuple-element.7), kind=kLoop, calls=%fused_computation.1 | loop fusion | flops 131072 | bytes 393216 | tf_op jit(solution)/shard_map/mul | solution.py:401
  80.7 0.0 copy-done.1
  80.7 0.0 copy-start
  80.7 0.7 convert_multiply_fusion
  81.4 0.3 copy-done
  81.7 0.7 copy.12
Async XLA Ops:
  79.0 1.7 %copy-start.1 = (bf16[128,512]{1,0:T(8,128)(2,1)S(1)}, bf16[128,512]{1,0:T(8,128)(2,1)}, u32[]{:S(2)}) copy-start(bf16[128,512]{1,0:T(8,128)(2,1)} %get-tuple-element.8) | copy-start | bytes 393220
  80.7 1.0 %copy-start = (bf16[256,512]{1,0:T(8,128)(2,1)S(1)}, bf16[256,512]{1,0:T(8,128)(2,1)}, u32[]{:S(2)}) copy-start(bf16[256,512]{1,0:T(8,128)(2,1)} %get-tuple-element.12) | copy-start | bytes 786436

commit v3 on v2

v3 whole, which is shorter than its diff:
```python
import functools
import math

import jax
import jax.numpy as jnp
from jax import lax
from jax.experimental import pallas as pl
from jax.experimental.pallas import tpu as pltpu
from jax.sharding import PartitionSpec as P

MESH = pl.DeviceIdType.MESH
BF16 = jnp.bfloat16
F32 = jnp.float32
X_HI, X_LO, CORES, NY, Z_IN = 2, 2, 2, 8, 4
HALF = NY // 2
GELU_C = math.sqrt(2.0 / math.pi)
N_SEM = 64


def dot(left, right):
    return jnp.dot(left, right, preferred_element_type=F32)


def dot_last(left, right):
    return lax.dot_general(left, right, (((1,), (1,)), ((), ())), preferred_element_type=F32)


def gelu_pair(pre, g_act):
    sq = pre * pre
    th = jnp.tanh(GELU_C * (pre + 0.044715 * sq * pre))
    half = 0.5 * (1.0 + th)
    slope = half + 0.5 * pre * (1.0 - th * th) * GELU_C * (1.0 + 3.0 * 0.044715 * sq)
    return (pre * half).astype(BF16), (g_act * slope).astype(BF16)


def kernel(
    nz, norm_factor,
    agg_ref, cot_ref, kin_ref, kout_ref, tiles_ref, cols_ref, count_ref,
    nodes_ref, gin_ref, gout_ref,
    rows_a, rows_c, at, ct, tiles, w_in, w_out, act, gpre, part, chain_out, chain_in, anti_out, fin_in,
    acc, back_out, back_in, halo_out, halo_in, pieces, piece_in, triple, triple_in, total,
    nodes_buf, gin_buf, gout_buf,
    s_sem, r_sem, l_sem,
):
    zg_n = nz // Z_IN
    npiece = X_HI * Z_IN
    nrow, feat = agg_ref.shape
    hid = kin_ref.shape[1]
    node, rep = lax.axis_index("node"), lax.axis_index("rep")
    core = lax.rem(node, CORES)
    z = lax.rem(lax.div(node, CORES), nz)
    xh = lax.div(node, CORES * nz)
    y, xl = lax.div(rep, X_LO), lax.rem(rep, X_LO)
    zg, zi = lax.div(z, Z_IN), lax.rem(z, Z_IN)
    other = 1 - core
    sign = 1 - 2 * core
    nodes = X_HI * nz * CORES

    def dev(xh, xl, y, z, core):
        return (xh * (nz * CORES) + z * CORES + core, y * X_LO + xl)

    def along_y(step, on_core):
        return dev(xh, xl, lax.rem(y + step + NY, NY), z, on_core)

    mate = dev(xh, xl, y, z, other)
    across = dev(lax.rem(xh + core, X_HI), 1 - xl, y, z, core)
    y_fwd, y_bwd = along_y(sign, core), along_y(-sign, core)
    nxt = (lax.rem(node + 1, nodes), rep)
    prv = (lax.rem(node + nodes - 1, nodes), rep)
    my_piece = xh * Z_IN + zi
    scatter_peers = []
    for j in range(1, npiece):
        pxh = lax.rem(xh + j // Z_IN, X_HI)
        pzi = lax.rem(zi + j % Z_IN, Z_IN)
        scatter_peers.append((j, dev(pxh, xl, y, zg * Z_IN + pzi, core), pxh * Z_IN + pzi))
    tri_peers = []
    for j in range(1, zg_n):
        tri_peers.append((j, dev(xh, xl, y, lax.rem(zg + j, zg_n) * Z_IN + zi, core)))

    barrier = pltpu.get_barrier_semaphore()
    peers = [y_fwd, y_bwd, across, mate, along_y(sign, other), along_y(-sign, other)]
    peers += [along_y(HALF, core), along_y(HALF, other), nxt, prv]
    peers += [d for _, d, _ in scatter_peers] + [d for _, d in tri_peers]
    for peer in peers:
        pl.semaphore_signal(barrier, inc=1, device_id=peer, device_id_type=MESH)

    def in_slot(slot):
        start = slot * hid
        return pl.ds(start if isinstance(slot, int) else pl.multiple_of(start, hid), hid)

    own, by_mate, by_x, by_x_mate = [pl.ds(k * nrow, nrow) for k in range(4)]
    near, far = pl.ds(0, 2 * nrow), pl.ds(2 * nrow, 2 * nrow)
    every = pl.ds(0, 4 * nrow)
    loads = [
        pltpu.make_async_copy(agg_ref, rows_a.at[own], l_sem.at[0]),
        pltpu.make_async_copy(cot_ref, rows_c.at[own], l_sem.at[1]),
        pltpu.make_async_copy(tiles_ref.at[0], tiles, l_sem.at[2]),
    ]
    shard_loads = [
        pltpu.make_async_copy(kin_ref, w_in.at[:, in_slot(0)], l_sem.at[3]),
        pltpu.make_async_copy(kout_ref, w_out.at[in_slot(0)], l_sem.at[4]),
    ]
    for load in loads:
        load.start()

    @pl.when(core == 0)
    def _():
        for load in shard_loads:
            load.start()

    pl.semaphore_wait(barrier, len(peers))

    started = []
    started_on = ([], [])
    used = [0]

    def ids(count=1):
        used[0] += count
        return used[0] - count

    def copy_to(src, dst, k, device, k_recv=None):
        return pltpu.make_async_remote_copy(
            src_ref=src, dst_ref=dst, send_sem=s_sem.at[k], recv_sem=r_sem.at[k if k_recv is None else k_recv],
            device_id=device, device_id_type=MESH,
        )

    def send(src, dst, k, device, k_recv=None):
        copy = copy_to(src, dst, k, device, k_recv)
        copy.start()
        started.append(copy)

    def send_on(only, make):
        make().start()
        started_on[only].append(make)

    def arrive(dst, k):
        copy_to(dst, dst, k, mate).wait_recv()

    k_win, k_wout = ids(HALF + 1), ids(HALF + 1)
    k_mate_rows, k_x_rows, k_fwd_rows = ids(2), ids(2), ids(2)
    k_chain = ids(2 * HALF)
    k_fin, k_fin_anti, k_fin_mate = ids(4), ids(2), ids()
    k_back = ids(3)
    k_halo = ids(2)
    k_piece, k_tri, k_tot, k_swap = ids(npiece), ids(zg_n), ids(npiece), ids()
    assert used[0] <= N_SEM

    def w_at(m, slot):
        return w_in.at[:, in_slot(slot)] if m == 0 else w_out.at[in_slot(slot)]

    def arrive_shard(m, j):
        arrive(w_at(m, j - core), (k_win, k_wout)[m] + j)

    def forward_shard(m, j):
        send(w_at(m, j - core), w_at(m, j + 1 - core), (k_win, k_wout)[m] + j + 1, y_fwd)

    send(kin_ref, w_at(0, other), k_win + 1, y_fwd)
    send(kout_ref, w_at(1, other), k_wout + 1, y_fwd)
    send(agg_ref, rows_a.at[by_x], k_x_rows, across)
    send(cot_ref, rows_c.at[by_x], k_x_rows + 1, across)
    send(agg_ref, rows_a.at[by_mate], k_mate_rows, mate)
    send(cot_ref, rows_c.at[by_mate], k_mate_rows + 1, mate)

    def flip(block):
        at[:, block] = rows_a[block].T
        ct[:, block] = rows_c[block].T

    def unit(slot, rows):
        a, g = gelu_pair(dot(rows_a[rows], w_in[:, in_slot(slot)]), dot_last(rows_c[rows], w_out[in_slot(slot)]))
        act[rows, in_slot(slot)] = a
        gpre[rows, in_slot(slot)] = g

    def weight_terms(slot, count=1):
        cols = pl.ds(slot * hid, count * hid)
        terms = (dot(at[...], gpre[:, cols]), dot(ct[...], act[:, cols]))
        for m in range(2):
            for k in range(count):
                part[slot + k, m] = terms[m][:, k * hid : (k + 1) * hid]

    for load in loads:
        load.wait()
    flip(own)
    arrive(rows_a.at[by_mate], k_mate_rows)
    arrive(rows_c.at[by_mate], k_mate_rows + 1)
    flip(by_mate)
    for m in range(2):
        arrive_shard(m, 1)
        forward_shard(m, 1)

    @pl.when(core == 0)
    def _():
        for load in shard_loads:
            load.wait()

    arrive(rows_a.at[by_x], k_x_rows)
    send(rows_a.at[by_x], rows_a.at[by_x_mate], k_fwd_rows, mate)
    unit(0, near)
    for m in range(2):
        arrive_shard(m, 2)
        forward_shard(m, 2)
    arrive(rows_c.at[by_x], k_x_rows + 1)
    send(rows_c.at[by_x], rows_c.at[by_x_mate], k_fwd_rows + 1, mate)
    unit(1, near)
    flip(by_x)
    arrive(rows_a.at[by_x_mate], k_fwd_rows)
    arrive(rows_c.at[by_x_mate], k_fwd_rows + 1)
    unit(0, far)
    unit(1, far)
    flip(by_x_mate)
    weight_terms(0, 2)

    @pl.when(core == 0)
    def _():
        anti_out[1] = part[0, 1].astype(BF16)
        send_on(0, lambda: copy_to(anti_out.at[1], fin_in.at[3], k_fin_mate, mate))

    def chain_start(only):
        for m in range(2):
            chain_out[HALF - 1, m] = part[HALF - 1 - only, m].astype(BF16)
            send_on(only, lambda m=m: copy_to(chain_out.at[HALF - 1, m], chain_in.at[HALF - 1, m], k_chain + 2 * (HALF - 1) + m, y_bwd))

    for m in range(2):
        arrive_shard(m, 3)

        @pl.when(core == 1)
        def _():
            send_on(1, lambda m=m: copy_to(w_at(m, 2), w_at(m, 3), (k_win, k_wout)[m] + HALF, y_fwd))

    unit(2, every)
    weight_terms(2)

    @pl.when(core == 1)
    def _():
        chain_start(1)
        for m in range(2):
            arrive(w_at(m, 3), (k_win, k_wout)[m] + HALF)

    unit(3, every)
    weight_terms(3)

    @pl.when(core == 0)
    def _():
        chain_start(0)

    @pl.when(core == 1)
    def _():
        for m in range(2):
            anti_out[m] = part[3, m].astype(BF16)
            send_on(1, lambda m=m: copy_to(anti_out.at[m], fin_in.at[2], k_fin_anti + m, along_y(HALF, m), k_fin_anti))

    def shares(block):
        return dot_last(gpre[block], w_in[...])

    def chain_step(k, m):
        arrive(chain_in.at[k + 1, m], k_chain + 2 * (k + 1) + m)
        chain_out[k, m] = (part[k - core, m] + chain_in[k + 1, m].astype(F32)).astype(BF16)
        if k > 1:
            send(chain_out.at[k, m], chain_in.at[k, m], k_chain + 2 * k + m, y_bwd)
        else:
            send(chain_out.at[k, m], fin_in.at[core], k_fin + 2 * m, along_y(-sign, m), k_fin + core)

    back_out[1] = shares(by_x_mate).astype(BF16)
    send(back_out.at[1], back_in.at[1], k_back + 1, mate)
    back_out[0] = shares(by_mate).astype(BF16)
    send(back_out.at[0], back_in.at[0], k_back, mate)
    for m in range(2):
        chain_step(2, m)
    acc[...] = shares(by_x)
    arrive(back_in.at[1], k_back + 1)
    back_out[2] = (acc[...] + back_in[1].astype(F32)).astype(BF16)
    send(back_out.at[2], back_in.at[2], k_back + 2, across)
    acc[...] = shares(own)
    for t in range(tiles.shape[0]):
        tiles[t] = tiles[t].T
    for m in range(2):
        chain_step(1, m)

    @pl.when(core == 1)
    def _():
        arrive(fin_in.at[3], k_fin_mate)

    @pl.when(core == 0)
    def _():
        fin_in[3] = part[0, 0].astype(BF16)

    arrive(fin_in.at[2], k_fin_anti)
    mine = fin_in[3].astype(F32) + fin_in[2].astype(F32)
    for c in range(2):
        arrive(fin_in.at[c], k_fin + c)
        mine = mine + fin_in[c].astype(F32)

    prow = feat // npiece
    for p in range(npiece):
        pieces[p] = mine[p * prow : (p + 1) * prow].astype(BF16)
    for j, peer, p in scatter_peers:
        send(pieces.at[p], piece_in.at[j], k_piece + j, peer)

    arrive(back_in.at[0], k_back)
    arrive(back_in.at[2], k_back + 2)
    g_agg = (acc[...] + back_in[0].astype(F32) + back_in[2].astype(F32)).astype(BF16)
    live_count = count_ref[0]
    sums = [None, None, None]
    for t in range(tiles.shape[0]):
        term = dot(tiles[t], g_agg)
        for k in range(3):
            on = jnp.logical_and(cols_ref[0, t] == k, t < live_count)
            add = term * jnp.where(on, 1.0, 0.0).astype(F32)
            sums[k] = add if sums[k] is None else sums[k] + add
    halo_out[0] = sums[0].astype(BF16)
    halo_out[1] = sums[2].astype(BF16)
    acc[...] = sums[1] + rows_c[own].astype(F32)
    send(halo_out.at[0], halo_in.at[0], k_halo, prv)
    send(halo_out.at[1], halo_in.at[1], k_halo + 1, nxt)

    tot = pieces[my_piece].astype(F32)
    for j, peer, _ in scatter_peers:
        arrive(piece_in.at[j], k_piece + j)
        tot = tot + piece_in[j].astype(F32)
    triple[...] = tot.astype(BF16)
    for j, peer in tri_peers:
        send(triple, triple_in.at[zg], k_tri + j, peer)
    triple_in[zg] = triple[...]

    arrive(halo_in.at[0], k_halo)
    arrive(halo_in.at[1], k_halo + 1)
    nodes_buf[...] = (acc[...] + halo_in[1].astype(F32) + halo_in[0].astype(F32)).astype(BF16)
    out_nodes = pltpu.make_async_copy(nodes_buf, nodes_ref, l_sem.at[0])
    out_nodes.start()

    for j, peer in tri_peers:
        arrive(triple_in.at[lax.rem(zg + zg_n - j, zg_n)], k_tri + j)
    tot = triple_in[0].astype(F32)
    for k in range(1, zg_n):
        tot = tot + triple_in[k].astype(F32)
    total[core, my_piece] = tot.astype(BF16)
    for j, peer, _ in scatter_peers:
        send(total.at[core, my_piece], total.at[core, my_piece], k_tot + j, peer)
    for j, peer, _ in scatter_peers:
        fxh = lax.rem(xh + X_HI - j // Z_IN, X_HI)
        fzi = lax.rem(zi + Z_IN - j % Z_IN, Z_IN)
        arrive(total.at[core, fxh * Z_IN + fzi], k_tot + j)
    send(total.at[core], total.at[core], k_swap, mate)
    arrive(total.at[other], k_swap)
    for p in range(npiece):
        gin_buf[p * prow : (p + 1) * prow, :] = total[0, p].astype(F32) * norm_factor
    out_gin = pltpu.make_async_copy(gin_buf, gin_ref, l_sem.at[1])
    out_gin.start()
    gout_buf[...] = jnp.concatenate([total[1, p] for p in range(npiece)], axis=0).T.astype(F32) * norm_factor
    out_gout = pltpu.make_async_copy(gout_buf, gout_ref, l_sem.at[2])
    out_gout.start()
    for copy in started:
        copy.wait_send()
    for only in range(2):

        @pl.when(core == only)
        def _():
            for make in started_on[only]:
                make().wait_send()

    out_nodes.wait()
    out_gin.wait()
    out_gout.wait()


def hand_over(*refs):
    n = len(refs) // 2
    copies = [pltpu.make_async_copy(refs[k], refs[n + k], refs[-1].at[k]) for k in range(n)]
    for copy in copies:
        copy.start()
    for copy in copies:
        copy.wait()


def local(nz, aggregated, cotangent, kernel_in, kernel_out, tile_values, tile_cols, tile_count):
    nrow, feat = aggregated.shape
    assert lax.axis_size("rep") == NY * X_LO
    hid = kernel_in.shape[1]
    slots = tile_values.shape[1]
    npiece = X_HI * Z_IN
    zg_n = nz // Z_IN
    prow = feat // npiece
    norm_factor = 1.0 / math.sqrt(nrow * lax.axis_size("node") * lax.axis_size("rep"))
    vmem = lambda shape, dtype=BF16: pltpu.VMEM(shape, dtype)
    hbm = pl.BlockSpec(memory_space=pltpu.HBM)
    scalars = pl.BlockSpec(memory_space=pltpu.SMEM)
    shapes = (
        jax.ShapeDtypeStruct((nrow, feat), BF16),
        jax.ShapeDtypeStruct((feat, hid), F32),
        jax.ShapeDtypeStruct((hid, feat), F32),
    )
    results = pl.pallas_call(
        functools.partial(kernel, nz, norm_factor),
        out_shape=shapes,
        in_specs=[hbm] * 5 + [scalars] * 2,
        out_specs=(hbm, hbm, hbm),
        scratch_shapes=[
            vmem((4 * nrow, feat)),
            vmem((4 * nrow, feat)),
            vmem((feat, 4 * nrow)),
            vmem((feat, 4 * nrow)),
            vmem((slots, nrow, nrow)),
            vmem((feat, HALF * hid)),
            vmem((HALF * hid, feat)),
            vmem((4 * nrow, HALF * hid)),
            vmem((4 * nrow, HALF * hid)),
            vmem((HALF, 2, feat, hid), F32),
            vmem((HALF, 2, feat, hid)),
            vmem((HALF, 2, feat, hid)),
            vmem((2, feat, hid)),
            vmem((4, feat, hid)),
            vmem((nrow, feat), F32),
            vmem((3, nrow, feat)),
            vmem((3, nrow, feat)),
            vmem((2, nrow, feat)),
            vmem((2, nrow, feat)),
            vmem((npiece, prow, hid)),
            vmem((npiece, prow, hid)),
            vmem((prow, hid)),
            vmem((zg_n, prow, hid)),
            vmem((2, npiece, prow, hid)),
            vmem((nrow, feat)),
            vmem((feat, hid), F32),
            vmem((hid, feat), F32),
            pltpu.SemaphoreType.DMA((N_SEM,)),
            pltpu.SemaphoreType.DMA((N_SEM,)),
            pltpu.SemaphoreType.DMA((5,)),
        ],
        compiler_params=pltpu.CompilerParams(
            collective_id=0, has_side_effects=True, vmem_limit_bytes=62 << 20
        ),
    )(aggregated, cotangent, kernel_in, kernel_out, tile_values, tile_cols, tile_count)
    return pl.pallas_call(
        hand_over,
        out_shape=shapes,
        in_specs=[hbm] * 3,
        out_specs=(hbm, hbm, hbm),
        scratch_shapes=[pltpu.SemaphoreType.DMA((3,))],
        compiler_params=pltpu.CompilerParams(vmem_limit_bytes=62 << 20),
    )(*results)


def solution(mesh):
    nz = mesh.shape["node"] // (X_HI * CORES)
    return jax.shard_map(
        functools.partial(local, nz),
        mesh=mesh,
        in_specs=(
            P(("node", "rep"), None),
            P(("node", "rep"), None),
            P(None, "rep"),
            P("rep", None),
            P(("node", "rep"), None, None, None),
            P(("node", "rep"), None),
            P(("node", "rep")),
        ),
        out_specs=(P(("node", "rep"), None), P(None, "rep"), P("rep", None)),
        check_vma=False,
    )
```

time: 82.6 us -> 100 us (1.21)
  Pallas kernels: 77.7 us -> 98.6 us
  other arithmetic: 2.4 us -> 0 us
    pallas_call x1 -> x2, Pallas kernels: 77.7 us -> 98.6 us  [the longest x1 73.7 us: local(): pl.pallas_call(functools.partial(kernel, nz, norm_factor), out_shape=shap...]
    mul x2 -> x0, other arithmetic: 2.4 us -> none  [the longest x1 1.66 us: local(): g_in.astype(F32) * norm_factor]
where the time goes in v3:
time: 100 us; the launch traced here: 99.9 us
  Pallas kernels  98.6 us (99%)
  between operations  1.29 us (1%)
    pallas_call x1, Pallas kernels, local(): pl.pallas_call(functools.partial(kernel, nz, norm_factor), out_shape=shap...  73.7 us
    pallas_call x1, Pallas kernels, local(): pl.pallas_call(hand_over, out_shape=shapes, in_specs=[hbm] * 3, out_specs...  25 us

profile of v3, /device:TPU:1, one launch (start us, length us, event | category | flops | bytes accessed | tf_op | source)
XLA Modules:
  0.0 99.9 jit_solution(5711532978080453052)
XLA Ops:
  1.3 73.7 %shard_map.94 = (bf16[256,512]{1,0:T(8,128)(2,1)}, f32[512,128]{1,0:T(8,128)}, f32[128,512]{1,0:T(8,128)}) custom-call(bf16[256,512]{1,0:T(8,128)(2,1)} %agg_ref.1, bf16[256,512]{1,0:T(8,128)(2,1)} %cot_ref.1, bf16[512,128]{1,0:T(8,128)(2,1)} %kin_ref.1, bf16[128,512]{1,0:T(8,128)(2,1)} %kout_ref.1, bf16[1,4,256,256]{3,2,1,0:T(8,128)(2,1)} %tiles_ref.1, ...), custom_call_target="tpu_custom_call" | custom-call | tf_op jit(solution)/shard_map/pallas_call | solution.py:391
  75.0 25.0 %shard_map.95 = (bf16[256,512]{1,0:T(8,128)(2,1)}, f32[512,128]{1,0:T(8,128)}, f32[128,512]{1,0:T(8,128)}) custom-call(bf16[256,512]{1,0:T(8,128)(2,1)} %get-tuple-element.6.refs_0_, f32[512,128]{1,0:T(8,128)} %get-tuple-element.7.refs_1_, f32[128,512]{1,0:T(8,128)} %get-tuple-element.8.refs_2_), custom_call_target="tpu_custom_call" | custom-call | tf_op jit(solution)/shard_map/pallas_call | solution.py:432

commit v4 on v3

--- a/solution.py
+++ b/solution.py
@@ -170,12 +170,9 @@
         act[rows, in_slot(slot)] = a
         gpre[rows, in_slot(slot)] = g
 
-    def weight_terms(slot, count=1):
-        cols = pl.ds(slot * hid, count * hid)
-        terms = (dot(at[...], gpre[:, cols]), dot(ct[...], act[:, cols]))
-        for m in range(2):
-            for k in range(count):
-                part[slot + k, m] = terms[m][:, k * hid : (k + 1) * hid]
+    def weight_term(slot, m):
+        left, right = (at, gpre) if m == 0 else (ct, act)
+        return dot(left[...], right[:, in_slot(slot)])
 
     for load in loads:
         load.wait()
@@ -186,102 +183,88 @@
     for m in range(2):
         arrive_shard(m, 1)
         forward_shard(m, 1)
+    unit(1 - core, near)
+    arrive(rows_a.at[by_x], k_x_rows)
+    send(rows_a.at[by_x], rows_a.at[by_x_mate], k_fwd_rows, mate)
+    for m in range(2):
+        arrive_shard(m, 2)
+        forward_shard(m, 2)
+    arrive(rows_c.at[by_x], k_x_rows + 1)
+    send(rows_c.at[by_x], rows_c.at[by_x_mate], k_fwd_rows + 1, mate)
+    unit(2 - core, near)
+    flip(by_x)
+    arrive(rows_a.at[by_x_mate], k_fwd_rows)
+    arrive(rows_c.at[by_x_mate], k_fwd_rows + 1)
+    flip(by_x_mate)
+    for m in range(2):
+        arrive_shard(m, 3)
+
+        @pl.when(core == 1)
+        def _():
+            send_on(1, lambda m=m: copy_to(w_at(m, 2), w_at(m, 3), (k_win, k_wout)[m] + HALF, y_fwd))
+
+    unit(3 - core, every)
+    for m in range(2):
+        chain_out[3, m] = weight_term(3 - core, m).astype(BF16)
+        send(chain_out.at[3, m], chain_in.at[3, m], k_chain + 6 + m, y_bwd)
+    for j in (2, 1):
+        unit(j - core, far)
+        for m in range(2):
+            part[j, m] = weight_term(j - core, m)
 
     @pl.when(core == 0)
     def _():
         for load in shard_loads:
             load.wait()
 
-    arrive(rows_a.at[by_x], k_x_rows)
-    send(rows_a.at[by_x], rows_a.at[by_x_mate], k_fwd_rows, mate)
-    unit(0, near)
-    for m in range(2):
-        arrive_shard(m, 2)
-        forward_shard(m, 2)
-    arrive(rows_c.at[by_x], k_x_rows + 1)
-    send(rows_c.at[by_x], rows_c.at[by_x_mate], k_fwd_rows + 1, mate)
-    unit(1, near)
-    flip(by_x)
-    arrive(rows_a.at[by_x_mate], k_fwd_rows)
-    arrive(rows_c.at[by_x_mate], k_fwd_rows + 1)
-    unit(0, far)
-    unit(1, far)
-    flip(by_x_mate)
-    weight_terms(0, 2)
-
-    @pl.when(core == 0)
-    def _():
-        anti_out[1] = part[0, 1].astype(BF16)
-        send_on(0, lambda: copy_to(anti_out.at[1], fin_in.at[3], k_fin_mate, mate))
-
-    def chain_start(only):
-        for m in range(2):
-            chain_out[HALF - 1, m] = part[HALF - 1 - only, m].astype(BF16)
-            send_on(only, lambda m=m: copy_to(chain_out.at[HALF - 1, m], chain_in.at[HALF - 1, m], k_chain + 2 * (HALF - 1) + m, y_bwd))
-
-    for m in range(2):
-        arrive_shard(m, 3)
-
-        @pl.when(core == 1)
-        def _():
-            send_on(1, lambda m=m: copy_to(w_at(m, 2), w_at(m, 3), (k_win, k_wout)[m] + HALF, y_fwd))
-
-    unit(2, every)
-    weight_terms(2)
-
-    @pl.when(core == 1)
-    def _():
-        chain_start(1)
-        for m in range(2):
-            arrive(w_at(m, 3), (k_win, k_wout)[m] + HALF)
-
-    unit(3, every)
-    weight_terms(3)
-
-    @pl.when(core == 0)
-    def _():
-        chain_start(0)
-
     @pl.when(core == 1)
     def _():
         for m in range(2):
-            anti_out[m] = part[3, m].astype(BF16)
+            arrive(w_at(m, 3), (k_win, k_wout)[m] + HALF)
+
+    unit(3 * core, every)
+    for m in range(2):
+        anti_out[m] = weight_term(3 * core, m).astype(BF16)
+
+        @pl.when(core == 1)
+        def _():
             send_on(1, lambda m=m: copy_to(anti_out.at[m], fin_in.at[2], k_fin_anti + m, along_y(HALF, m), k_fin_anti))
+
+    @pl.when(core == 0)
+    def _():
+        send_on(0, lambda: copy_to(anti_out.at[1], fin_in.at[3], k_fin_mate, mate))
+        fin_in[3] = anti_out[0]
 
     def shares(block):
         return dot_last(gpre[block], w_in[...])
 
     def chain_step(k, m):
         arrive(chain_in.at[k + 1, m], k_chain + 2 * (k + 1) + m)
-        chain_out[k, m] = (part[k - core, m] + chain_in[k + 1, m].astype(F32)).astype(BF16)
+        chain_out[k, m] = (part[k, m] + chain_in[k + 1, m].astype(F32)).astype(BF16)
         if k > 1:
             send(chain_out.at[k, m], chain_in.at[k, m], k_chain + 2 * k + m, y_bwd)
         else:
             send(chain_out.at[k, m], fin_in.at[core], k_fin + 2 * m, along_y(-sign, m), k_fin + core)
 
+    for m in range(2):
+        chain_step(2, m)
     back_out[1] = shares(by_x_mate).astype(BF16)
     send(back_out.at[1], back_in.at[1], k_back + 1, mate)
     back_out[0] = shares(by_mate).astype(BF16)
     send(back_out.at[0], back_in.at[0], k_back, mate)
-    for m in range(2):
-        chain_step(2, m)
     acc[...] = shares(by_x)
     arrive(back_in.at[1], k_back + 1)
     back_out[2] = (acc[...] + back_in[1].astype(F32)).astype(BF16)
     send(back_out.at[2], back_in.at[2], k_back + 2, across)
+    for m in range(2):
+        chain_step(1, m)
     acc[...] = shares(own)
     for t in range(tiles.shape[0]):
         tiles[t] = tiles[t].T
-    for m in range(2):
-        chain_step(1, m)
 
     @pl.when(core == 1)
     def _():
         arrive(fin_in.at[3], k_fin_mate)
-
-    @pl.when(core == 0)
-    def _():
-        fin_in[3] = part[0, 0].astype(BF16)
 
     arrive(fin_in.at[2], k_fin_anti)
     mine = fin_in[3].astype(F32) + fin_in[2].astype(F32)
@@ -363,11 +346,16 @@
 
 
 def hand_over(*refs):
-    n = len(refs) // 2
-    copies = [pltpu.make_async_copy(refs[k], refs[n + k], refs[-1].at[k]) for k in range(n)]
-    for copy in copies:
+    n = len(refs) // 3
+    sems = refs[-1]
+    fetch = [pltpu.make_async_copy(refs[k], refs[2 * n + k], sems.at[k]) for k in range(n)]
+    store = [pltpu.make_async_copy(refs[2 * n + k], refs[n + k], sems.at[n + k]) for k in range(n)]
+    for copy in fetch:
         copy.start()
-    for copy in copies:
+    for k in range(n):
+        fetch[k].wait()
+        store[k].start()
+    for copy in store:
         copy.wait()
 
 
@@ -434,7 +422,7 @@
         out_shape=shapes,
         in_specs=[hbm] * 3,
         out_specs=(hbm, hbm, hbm),
-        scratch_shapes=[pltpu.SemaphoreType.DMA((3,))],
+        scratch_shapes=[vmem(s.shape, s.dtype) for s in shapes] + [pltpu.SemaphoreType.DMA((6,))],
         compiler_params=pltpu.CompilerParams(vmem_limit_bytes=62 << 20),
     )(*results)
 

time: 100 us -> 75.2 us (0.75)
  Pallas kernels: 98.6 us -> 73.7 us
    pallas_call x1, Pallas kernels: 25 us -> 1.88 us  [local(): pl.pallas_call(hand_over, out_shape=shapes, in_specs=[hbm] * 3, out_specs...]
    pallas_call x1, Pallas kernels: 73.7 us -> 71.8 us  [local(): pl.pallas_call(functools.partial(kernel, nz, norm_factor), out_shape=shap...]
where the time goes in v4:
time: 75.2 us; the launch traced here: 75 us
  Pallas kernels  73.7 us (98%)
  between operations  1.29 us (2%)
    pallas_call x1, Pallas kernels, local(): pl.pallas_call(functools.partial(kernel, nz, norm_factor), out_shape=shap...  71.8 us
    pallas_call x1, Pallas kernels, local(): pl.pallas_call(hand_over, out_shape=shapes, in_specs=[hbm] * 3, out_specs...  1.88 us

profile of v4, /device:TPU:1, one launch (start us, length us, event | category | flops | bytes accessed | tf_op | source)
XLA Modules:
  0.0 75.0 jit_solution(2358219417349291243)
XLA Ops:
  1.3 71.8 %shard_map.94 = (bf16[256,512]{1,0:T(8,128)(2,1)}, f32[512,128]{1,0:T(8,128)}, f32[128,512]{1,0:T(8,128)}) custom-call(bf16[256,512]{1,0:T(8,128)(2,1)} %agg_ref.1, bf16[256,512]{1,0:T(8,128)(2,1)} %cot_ref.1, bf16[512,128]{1,0:T(8,128)(2,1)} %kin_ref.1, bf16[128,512]{1,0:T(8,128)(2,1)} %kout_ref.1, bf16[1,4,256,256]{3,2,1,0:T(8,128)(2,1)} %tiles_ref.1, ...), custom_call_target="tpu_custom_call" | custom-call | tf_op jit(solution)/shard_map/pallas_call | solution.py:379
  73.1 1.9 %shard_map.95 = (bf16[256,512]{1,0:T(8,128)(2,1)}, f32[512,128]{1,0:T(8,128)}, f32[128,512]{1,0:T(8,128)}) custom-call(bf16[256,512]{1,0:T(8,128)(2,1)} %get-tuple-element.6.refs_0_, f32[512,128]{1,0:T(8,128)} %get-tuple-element.7.refs_1_, f32[128,512]{1,0:T(8,128)} %get-tuple-element.8.refs_2_), custom_call_target="tpu_custom_call" | custom-call | tf_op jit(solution)/shard_map/pallas_call | solution.py:420

commit v5 on v4

--- a/solution.py
+++ b/solution.py
@@ -14,7 +14,8 @@
 X_HI, X_LO, CORES, NY, Z_IN = 2, 2, 2, 8, 4
 HALF = NY // 2
 GELU_C = math.sqrt(2.0 / math.pi)
-N_SEM = 64
+N_SEM = 96
+CUTS = 2
 
 
 def dot(left, right):
@@ -136,26 +137,34 @@
     def arrive(dst, k):
         copy_to(dst, dst, k, mate).wait_recv()
 
-    k_win, k_wout = ids(HALF + 1), ids(HALF + 1)
+    k_shard = [ids((HALF + 1) * CUTS) for _ in range(2)]
     k_mate_rows, k_x_rows, k_fwd_rows = ids(2), ids(2), ids(2)
-    k_chain = ids(2 * HALF)
-    k_fin, k_fin_anti, k_fin_mate = ids(4), ids(2), ids()
+    k_chain = ids(HALF * 2 * CUTS)
+    k_fin, k_fin_anti, k_fin_mate = ids(4 * CUTS), ids(2), ids()
     k_back = ids(3)
     k_halo = ids(2)
     k_piece, k_tri, k_tot, k_swap = ids(npiece), ids(zg_n), ids(npiece), ids()
     assert used[0] <= N_SEM
 
-    def w_at(m, slot):
-        return w_in.at[:, in_slot(slot)] if m == 0 else w_out.at[in_slot(slot)]
-
-    def arrive_shard(m, j):
-        arrive(w_at(m, j - core), (k_win, k_wout)[m] + j)
-
-    def forward_shard(m, j):
-        send(w_at(m, j - core), w_at(m, j + 1 - core), (k_win, k_wout)[m] + j + 1, y_fwd)
-
-    send(kin_ref, w_at(0, other), k_win + 1, y_fwd)
-    send(kout_ref, w_at(1, other), k_wout + 1, y_fwd)
+    def w_at(m, slot, h):
+        if m == 0:
+            return w_in.at[pl.ds(h * (feat // CUTS), feat // CUTS), in_slot(slot)]
+        size = hid // CUTS
+        start = slot * hid + h * size
+        return w_out.at[pl.ds(start if isinstance(slot, int) else pl.multiple_of(start, size), size)]
+
+    pieces_of = [(m, h) for m in range(2) for h in range(CUTS)]
+
+    def arrive_shard(m, h, j, slot):
+        arrive(w_at(m, slot, h), k_shard[m] + j * CUTS + h)
+
+    def forward_shard(m, h, j):
+        send(w_at(m, j - core, h), w_at(m, j + 1 - core, h), k_shard[m] + (j + 1) * CUTS + h, y_fwd)
+
+    for m, h in pieces_of:
+        shard = (kin_ref, kout_ref)[m]
+        size = shard.shape[0] // CUTS
+        send(shard.at[pl.ds(h * size, size)], w_at(m, other, h), k_shard[m] + CUTS + h, y_fwd)
     send(agg_ref, rows_a.at[by_x], k_x_rows, across)
     send(cot_ref, rows_c.at[by_x], k_x_rows + 1, across)
     send(agg_ref, rows_a.at[by_mate], k_mate_rows, mate)
@@ -180,15 +189,15 @@
     arrive(rows_a.at[by_mate], k_mate_rows)
     arrive(rows_c.at[by_mate], k_mate_rows + 1)
     flip(by_mate)
-    for m in range(2):
-        arrive_shard(m, 1)
-        forward_shard(m, 1)
+    for m, h in pieces_of:
+        arrive_shard(m, h, 1, 1 - core)
+        forward_shard(m, h, 1)
     unit(1 - core, near)
     arrive(rows_a.at[by_x], k_x_rows)
     send(rows_a.at[by_x], rows_a.at[by_x_mate], k_fwd_rows, mate)
-    for m in range(2):
-        arrive_shard(m, 2)
-        forward_shard(m, 2)
+    for m, h in pieces_of:
+        arrive_shard(m, h, 2, 2 - core)
+        forward_shard(m, h, 2)
     arrive(rows_c.at[by_x], k_x_rows + 1)
     send(rows_c.at[by_x], rows_c.at[by_x_mate], k_fwd_rows + 1, mate)
     unit(2 - core, near)
@@ -196,17 +205,24 @@
     arrive(rows_a.at[by_x_mate], k_fwd_rows)
     arrive(rows_c.at[by_x_mate], k_fwd_rows + 1)
     flip(by_x_mate)
-    for m in range(2):
-        arrive_shard(m, 3)
+    for m, h in pieces_of:
+        arrive_shard(m, h, 3, 3 - core)
 
         @pl.when(core == 1)
         def _():
-            send_on(1, lambda m=m: copy_to(w_at(m, 2), w_at(m, 3), (k_win, k_wout)[m] + HALF, y_fwd))
+            send_on(1, lambda m=m, h=h: copy_to(w_at(m, 2, h), w_at(m, 3, h), k_shard[m] + HALF * CUTS + h, y_fwd))
+
+    def rows_of(h):
+        return pl.ds(h * (feat // CUTS), feat // CUTS)
+
+    def k_link(k, m, h):
+        return k_chain + (k * 2 + m) * CUTS + h
 
     unit(3 - core, every)
     for m in range(2):
         chain_out[3, m] = weight_term(3 - core, m).astype(BF16)
-        send(chain_out.at[3, m], chain_in.at[3, m], k_chain + 6 + m, y_bwd)
+        for h in range(CUTS):
+            send(chain_out.at[3, m, rows_of(h)], chain_in.at[3, m, rows_of(h)], k_link(3, m, h), y_bwd)
     for j in (2, 1):
         unit(j - core, far)
         for m in range(2):
@@ -219,8 +235,8 @@
 
     @pl.when(core == 1)
     def _():
-        for m in range(2):
-            arrive(w_at(m, 3), (k_win, k_wout)[m] + HALF)
+        for m, h in pieces_of:
+            arrive_shard(m, h, HALF, 3)
 
     unit(3 * core, every)
     for m in range(2):
@@ -238,16 +254,18 @@
     def shares(block):
         return dot_last(gpre[block], w_in[...])
 
-    def chain_step(k, m):
-        arrive(chain_in.at[k + 1, m], k_chain + 2 * (k + 1) + m)
-        chain_out[k, m] = (part[k, m] + chain_in[k + 1, m].astype(F32)).astype(BF16)
+    def chain_step(k, m, h):
+        cut = rows_of(h)
+        arrive(chain_in.at[k + 1, m, cut], k_link(k + 1, m, h))
+        chain_out[k, m, cut] = (part[k, m, cut] + chain_in[k + 1, m, cut].astype(F32)).astype(BF16)
         if k > 1:
-            send(chain_out.at[k, m], chain_in.at[k, m], k_chain + 2 * k + m, y_bwd)
+            send(chain_out.at[k, m, cut], chain_in.at[k, m, cut], k_link(k, m, h), y_bwd)
         else:
-            send(chain_out.at[k, m], fin_in.at[core], k_fin + 2 * m, along_y(-sign, m), k_fin + core)
-
-    for m in range(2):
-        chain_step(2, m)
+            to = along_y(-sign, m)
+            send(chain_out.at[k, m, cut], fin_in.at[core, cut], k_fin + (2 + m) * CUTS + h, to, k_fin + core * CUTS + h)
+
+    for m, h in pieces_of:
+        chain_step(2, m, h)
     back_out[1] = shares(by_x_mate).astype(BF16)
     send(back_out.at[1], back_in.at[1], k_back + 1, mate)
     back_out[0] = shares(by_mate).astype(BF16)
@@ -256,8 +274,8 @@
     arrive(back_in.at[1], k_back + 1)
     back_out[2] = (acc[...] + back_in[1].astype(F32)).astype(BF16)
     send(back_out.at[2], back_in.at[2], k_back + 2, across)
-    for m in range(2):
-        chain_step(1, m)
+    for m, h in pieces_of:
+        chain_step(1, m, h)
     acc[...] = shares(own)
     for t in range(tiles.shape[0]):
         tiles[t] = tiles[t].T
@@ -269,7 +287,8 @@
     arrive(fin_in.at[2], k_fin_anti)
     mine = fin_in[3].astype(F32) + fin_in[2].astype(F32)
     for c in range(2):
-        arrive(fin_in.at[c], k_fin + c)
+        for h in range(CUTS):
+            arrive(fin_in.at[c, rows_of(h)], k_fin + c * CUTS + h)
         mine = mine + fin_in[c].astype(F32)
 
     prow = feat // npiece

time: 75.2 us -> 74.5 us (level)
  no operation moved by 1% of the time
where the time goes in v5:
time: 74.5 us; the launch traced here: 74.3 us
  Pallas kernels  73 us (98%)
  between operations  1.29 us (2%)
    pallas_call x1, Pallas kernels, local(): pl.pallas_call(functools.partial(kernel, nz, norm_factor), out_shape=shap...  71.1 us
    pallas_call x1, Pallas kernels, local(): pl.pallas_call(hand_over, out_shape=shapes, in_specs=[hbm] * 3, out_specs...  1.88 us

profile of v5, /device:TPU:1, one launch (start us, length us, event | category | flops | bytes accessed | tf_op | source)
XLA Modules:
  0.0 74.3 jit_solution(148783405949644545)
XLA Ops:
  1.3 71.1 %shard_map.94 = (bf16[256,512]{1,0:T(8,128)(2,1)}, f32[512,128]{1,0:T(8,128)}, f32[128,512]{1,0:T(8,128)}) custom-call(bf16[256,512]{1,0:T(8,128)(2,1)} %agg_ref.1, bf16[256,512]{1,0:T(8,128)(2,1)} %cot_ref.1, bf16[512,128]{1,0:T(8,128)(2,1)} %kin_ref.1, bf16[128,512]{1,0:T(8,128)(2,1)} %kout_ref.1, bf16[1,4,256,256]{3,2,1,0:T(8,128)(2,1)} %tiles_ref.1, ...), custom_call_target="tpu_custom_call" | custom-call | tf_op jit(solution)/shard_map/pallas_call | solution.py:398
  72.4 1.9 %shard_map.95 = (bf16[256,512]{1,0:T(8,128)(2,1)}, f32[512,128]{1,0:T(8,128)}, f32[128,512]{1,0:T(8,128)}) custom-call(bf16[256,512]{1,0:T(8,128)(2,1)} %get-tuple-element.6.refs_0_, f32[512,128]{1,0:T(8,128)} %get-tuple-element.7.refs_1_, f32[128,512]{1,0:T(8,128)} %get-tuple-element.8.refs_2_), custom_call_target="tpu_custom_call" | custom-call | tf_op jit(solution)/shard_map/pallas_call | solution.py:439

commit v6 on v5

--- a/solution.py
+++ b/solution.py
@@ -39,7 +39,7 @@
     agg_ref, cot_ref, kin_ref, kout_ref, tiles_ref, cols_ref, count_ref,
     nodes_ref, gin_ref, gout_ref,
     rows_a, rows_c, at, ct, tiles, w_in, w_out, act, gpre, part, chain_out, chain_in, anti_out, fin_in,
-    acc, back_out, back_in, halo_out, halo_in, pieces, piece_in, triple, triple_in, total,
+    shares, sums, g_agg, back_out, back_in, halo_out, halo_in, pieces, piece_in, triple, triple_in, total,
     nodes_buf, gin_buf, gout_buf,
     s_sem, r_sem, l_sem,
 ):
@@ -90,8 +90,6 @@
         return pl.ds(start if isinstance(slot, int) else pl.multiple_of(start, hid), hid)
 
     own, by_mate, by_x, by_x_mate = [pl.ds(k * nrow, nrow) for k in range(4)]
-    near, far = pl.ds(0, 2 * nrow), pl.ds(2 * nrow, 2 * nrow)
-    every = pl.ds(0, 4 * nrow)
     loads = [
         pltpu.make_async_copy(agg_ref, rows_a.at[own], l_sem.at[0]),
         pltpu.make_async_copy(cot_ref, rows_c.at[own], l_sem.at[1]),
@@ -170,18 +168,40 @@
     send(agg_ref, rows_a.at[by_mate], k_mate_rows, mate)
     send(cot_ref, rows_c.at[by_mate], k_mate_rows + 1, mate)
 
+    def chunks(count, size, body):
+        def step(i, carry):
+            body(pl.ds(pl.multiple_of(i * size, size), size))
+            return carry
+
+        lax.fori_loop(0, count, step, 0)
+
     def flip(block):
-        at[:, block] = rows_a[block].T
-        ct[:, block] = rows_c[block].T
-
-    def unit(slot, rows):
-        a, g = gelu_pair(dot(rows_a[rows], w_in[:, in_slot(slot)]), dot_last(rows_c[rows], w_out[in_slot(slot)]))
-        act[rows, in_slot(slot)] = a
-        gpre[rows, in_slot(slot)] = g
-
-    def weight_term(slot, m):
+        def body(cols):
+            at[cols, block] = rows_a[block, cols].T
+            ct[cols, block] = rows_c[block, cols].T
+
+        chunks(feat // hid, hid, body)
+
+    def unit(slot, first, count):
+        cols = in_slot(slot)
+
+        def step(i, carry):
+            rows = pl.ds(pl.multiple_of(i * nrow, nrow), nrow)
+            a, g = gelu_pair(dot(rows_a[rows], w_in[:, cols]), dot_last(rows_c[rows], w_out[cols]))
+            act[rows, cols] = a
+            gpre[rows, cols] = g
+            return carry
+
+        lax.fori_loop(first, first + count, step, 0)
+
+    def weight_term(slot, m, dst):
         left, right = (at, gpre) if m == 0 else (ct, act)
-        return dot(left[...], right[:, in_slot(slot)])
+        cols = in_slot(slot)
+
+        def body(rows):
+            dst[rows] = dot(left[rows], right[:, cols]).astype(dst.dtype)
+
+        chunks(2, feat // 2, body)
 
     for load in loads:
         load.wait()
@@ -192,7 +212,7 @@
     for m, h in pieces_of:
         arrive_shard(m, h, 1, 1 - core)
         forward_shard(m, h, 1)
-    unit(1 - core, near)
+    unit(1 - core, 0, 2)
     arrive(rows_a.at[by_x], k_x_rows)
     send(rows_a.at[by_x], rows_a.at[by_x_mate], k_fwd_rows, mate)
     for m, h in pieces_of:
@@ -200,7 +220,7 @@
         forward_shard(m, h, 2)
     arrive(rows_c.at[by_x], k_x_rows + 1)
     send(rows_c.at[by_x], rows_c.at[by_x_mate], k_fwd_rows + 1, mate)
-    unit(2 - core, near)
+    unit(2 - core, 0, 2)
     flip(by_x)
     arrive(rows_a.at[by_x_mate], k_fwd_rows)
     arrive(rows_c.at[by_x_mate], k_fwd_rows + 1)
@@ -218,15 +238,15 @@
     def k_link(k, m, h):
         return k_chain + (k * 2 + m) * CUTS + h
 
-    unit(3 - core, every)
+    unit(3 - core, 0, 4)
     for m in range(2):
-        chain_out[3, m] = weight_term(3 - core, m).astype(BF16)
+        weight_term(3 - core, m, chain_out.at[3, m])
         for h in range(CUTS):
             send(chain_out.at[3, m, rows_of(h)], chain_in.at[3, m, rows_of(h)], k_link(3, m, h), y_bwd)
     for j in (2, 1):
-        unit(j - core, far)
+        unit(j - core, 2, 2)
         for m in range(2):
-            part[j, m] = weight_term(j - core, m)
+            weight_term(j - core, m, part.at[j, m])
 
     @pl.when(core == 0)
     def _():
@@ -238,9 +258,9 @@
         for m, h in pieces_of:
             arrive_shard(m, h, HALF, 3)
 
-    unit(3 * core, every)
+    unit(3 * core, 0, 4)
     for m in range(2):
-        anti_out[m] = weight_term(3 * core, m).astype(BF16)
+        weight_term(3 * core, m, anti_out.at[m])
 
         @pl.when(core == 1)
         def _():
@@ -250,9 +270,6 @@
     def _():
         send_on(0, lambda: copy_to(anti_out.at[1], fin_in.at[3], k_fin_mate, mate))
         fin_in[3] = anti_out[0]
-
-    def shares(block):
-        return dot_last(gpre[block], w_in[...])
 
     def chain_step(k, m, h):
         cut = rows_of(h)
@@ -266,19 +283,20 @@
 
     for m, h in pieces_of:
         chain_step(2, m, h)
-    back_out[1] = shares(by_x_mate).astype(BF16)
+    def share(rows):
+        shares[rows] = dot_last(gpre[rows], w_in[...])
+
+    chunks(4, nrow, share)
+    back_out[1] = shares[by_x_mate].astype(BF16)
     send(back_out.at[1], back_in.at[1], k_back + 1, mate)
-    back_out[0] = shares(by_mate).astype(BF16)
+    back_out[0] = shares[by_mate].astype(BF16)
     send(back_out.at[0], back_in.at[0], k_back, mate)
-    acc[...] = shares(by_x)
     arrive(back_in.at[1], k_back + 1)
-    back_out[2] = (acc[...] + back_in[1].astype(F32)).astype(BF16)
+    back_out[2] = (shares[by_x] + back_in[1].astype(F32)).astype(BF16)
     send(back_out.at[2], back_in.at[2], k_back + 2, across)
     for m, h in pieces_of:
         chain_step(1, m, h)
-    acc[...] = shares(own)
-    for t in range(tiles.shape[0]):
-        tiles[t] = tiles[t].T
+    sums[...] = jnp.zeros_like(sums)
 
     @pl.when(core == 1)
     def _():
@@ -299,18 +317,19 @@
 
     arrive(back_in.at[0], k_back)
     arrive(back_in.at[2], k_back + 2)
-    g_agg = (acc[...] + back_in[0].astype(F32) + back_in[2].astype(F32)).astype(BF16)
+    g_agg[...] = (shares[own] + back_in[0].astype(F32) + back_in[2].astype(F32)).astype(BF16)
     live_count = count_ref[0]
-    sums = [None, None, None]
-    for t in range(tiles.shape[0]):
-        term = dot(tiles[t], g_agg)
+
+    def add_tile(t, carry):
+        term = dot(tiles[t].T, g_agg[...])
         for k in range(3):
             on = jnp.logical_and(cols_ref[0, t] == k, t < live_count)
-            add = term * jnp.where(on, 1.0, 0.0).astype(F32)
-            sums[k] = add if sums[k] is None else sums[k] + add
+            sums[k] += term * jnp.where(on, 1.0, 0.0).astype(F32)
+        return carry
+
+    lax.fori_loop(0, tiles.shape[0], add_tile, 0)
     halo_out[0] = sums[0].astype(BF16)
     halo_out[1] = sums[2].astype(BF16)
-    acc[...] = sums[1] + rows_c[own].astype(F32)
     send(halo_out.at[0], halo_in.at[0], k_halo, prv)
     send(halo_out.at[1], halo_in.at[1], k_halo + 1, nxt)
 
@@ -325,7 +344,8 @@
 
     arrive(halo_in.at[0], k_halo)
     arrive(halo_in.at[1], k_halo + 1)
-    nodes_buf[...] = (acc[...] + halo_in[1].astype(F32) + halo_in[0].astype(F32)).astype(BF16)
+    centre = sums[1] + rows_c[own].astype(F32)
+    nodes_buf[...] = (centre + halo_in[1].astype(F32) + halo_in[0].astype(F32)).astype(BF16)
     out_nodes = pltpu.make_async_copy(nodes_buf, nodes_ref, l_sem.at[0])
     out_nodes.start()
 
@@ -415,7 +435,9 @@
             vmem((HALF, 2, feat, hid)),
             vmem((2, feat, hid)),
             vmem((4, feat, hid)),
-            vmem((nrow, feat), F32),
+            vmem((4 * nrow, feat), F32),
+            vmem((3, nrow, feat), F32),
+            vmem((nrow, feat)),
             vmem((3, nrow, feat)),
             vmem((3, nrow, feat)),
             vmem((2, nrow, feat)),

time: 74.5 us -> 76.1 us (1.021)
  Pallas kernels: 73 us -> 74.6 us
    pallas_call x1, Pallas kernels: 71.1 us -> 72.7 us  [local(): pl.pallas_call(functools.partial(kernel, nz, norm_factor), out_shape=shap...]
where the time goes in v6:
time: 76.1 us; the launch traced here: 75.9 us
  Pallas kernels  74.6 us (98%)
  between operations  1.29 us (2%)
    pallas_call x1, Pallas kernels, local(): pl.pallas_call(functools.partial(kernel, nz, norm_factor), out_shape=shap...  72.7 us
    pallas_call x1, Pallas kernels, local(): pl.pallas_call(hand_over, out_shape=shapes, in_specs=[hbm] * 3, out_specs...  1.88 us

profile of v6, /device:TPU:1, one launch (start us, length us, event | category | flops | bytes accessed | tf_op | source)
XLA Modules:
  0.0 75.9 jit_solution(1432551340865897856)
XLA Ops:
  1.3 72.7 %shard_map.94 = (bf16[256,512]{1,0:T(8,128)(2,1)}, f32[512,128]{1,0:T(8,128)}, f32[128,512]{1,0:T(8,128)}) custom-call(bf16[256,512]{1,0:T(8,128)(2,1)} %agg_ref.1, bf16[256,512]{1,0:T(8,128)(2,1)} %cot_ref.1, bf16[512,128]{1,0:T(8,128)(2,1)} %kin_ref.1, bf16[128,512]{1,0:T(8,128)(2,1)} %kout_ref.1, bf16[1,4,256,256]{3,2,1,0:T(8,128)(2,1)} %tiles_ref.1, ...), custom_call_target="tpu_custom_call" | custom-call | tf_op jit(solution)/shard_map/pallas_call | solution.py:418
  74.0 1.9 %shard_map.95 = (bf16[256,512]{1,0:T(8,128)(2,1)}, f32[512,128]{1,0:T(8,128)}, f32[128,512]{1,0:T(8,128)}) custom-call(bf16[256,512]{1,0:T(8,128)(2,1)} %get-tuple-element.6.refs_0_, f32[512,128]{1,0:T(8,128)} %get-tuple-element.7.refs_1_, f32[128,512]{1,0:T(8,128)} %get-tuple-element.8.refs_2_), custom_call_target="tpu_custom_call" | custom-call | tf_op jit(solution)/shard_map/pallas_call | solution.py:461

commit v7 on v5

--- a/solution.py
+++ b/solution.py
@@ -70,7 +70,7 @@
     prv = (lax.rem(node + nodes - 1, nodes), rep)
     my_piece = xh * Z_IN + zi
     scatter_peers = []
-    for j in range(1, npiece):
+    for j in range(npiece - 1, 0, -1):
         pxh = lax.rem(xh + j // Z_IN, X_HI)
         pzi = lax.rem(zi + j % Z_IN, Z_IN)
         scatter_peers.append((j, dev(pxh, xl, y, zg * Z_IN + pzi, core), pxh * Z_IN + pzi))
@@ -134,6 +134,19 @@
         make().start()
         started_on[only].append(make)
 
+    def settle():
+        for copy in started:
+            copy.wait_send()
+        started.clear()
+        for only in range(2):
+
+            @pl.when(core == only)
+            def _():
+                for make in started_on[only]:
+                    make().wait_send()
+
+            started_on[only].clear()
+
     def arrive(dst, k):
         copy_to(dst, dst, k, mate).wait_recv()
 
@@ -242,10 +255,6 @@
     for m in range(2):
         anti_out[m] = weight_term(3 * core, m).astype(BF16)
 
-        @pl.when(core == 1)
-        def _():
-            send_on(1, lambda m=m: copy_to(anti_out.at[m], fin_in.at[2], k_fin_anti + m, along_y(HALF, m), k_fin_anti))
-
     @pl.when(core == 0)
     def _():
         send_on(0, lambda: copy_to(anti_out.at[1], fin_in.at[3], k_fin_mate, mate))
@@ -266,6 +275,12 @@
 
     for m, h in pieces_of:
         chain_step(2, m, h)
+
+    @pl.when(core == 1)
+    def _():
+        for m in range(2):
+            send_on(1, lambda m=m: copy_to(anti_out.at[m], fin_in.at[2], k_fin_anti + m, along_y(HALF, m), k_fin_anti))
+
     back_out[1] = shares(by_x_mate).astype(BF16)
     send(back_out.at[1], back_in.at[1], k_back + 1, mate)
     back_out[0] = shares(by_mate).astype(BF16)
@@ -311,6 +326,7 @@
     halo_out[0] = sums[0].astype(BF16)
     halo_out[1] = sums[2].astype(BF16)
     acc[...] = sums[1] + rows_c[own].astype(F32)
+    settle()
     send(halo_out.at[0], halo_in.at[0], k_halo, prv)
     send(halo_out.at[1], halo_in.at[1], k_halo + 1, nxt)
 
@@ -352,13 +368,6 @@
     out_gout.start()
     for copy in started:
         copy.wait_send()
-    for only in range(2):
-
-        @pl.when(core == only)
-        def _():
-            for make in started_on[only]:
-                make().wait_send()
-
     out_nodes.wait()
     out_gin.wait()
     out_gout.wait()

time: 74.5 us -> 74.3 us (level)
  no operation moved by 1% of the time
where the time goes in v7:
time: 74.3 us; the launch traced here: 74.1 us
  Pallas kernels  72.8 us (98%)
  between operations  1.29 us (2%)
    pallas_call x1, Pallas kernels, local(): pl.pallas_call(functools.partial(kernel, nz, norm_factor), out_shape=shap...  70.9 us
    pallas_call x1, Pallas kernels, local(): pl.pallas_call(hand_over, out_shape=shapes, in_specs=[hbm] * 3, out_specs...  1.88 us

profile of v7, /device:TPU:1, one launch (start us, length us, event | category | flops | bytes accessed | tf_op | source)
XLA Modules:
  0.0 74.1 jit_solution(13816973405289916094)
XLA Ops:
  1.3 70.9 %shard_map.94 = (bf16[256,512]{1,0:T(8,128)(2,1)}, f32[512,128]{1,0:T(8,128)}, f32[128,512]{1,0:T(8,128)}) custom-call(bf16[256,512]{1,0:T(8,128)(2,1)} %agg_ref.1, bf16[256,512]{1,0:T(8,128)(2,1)} %cot_ref.1, bf16[512,128]{1,0:T(8,128)(2,1)} %kin_ref.1, bf16[128,512]{1,0:T(8,128)(2,1)} %kout_ref.1, bf16[1,4,256,256]{3,2,1,0:T(8,128)(2,1)} %tiles_ref.1, ...), custom_call_target="tpu_custom_call" | custom-call | tf_op jit(solution)/shard_map/pallas_call | solution.py:407
  72.2 1.9 %shard_map.95 = (bf16[256,512]{1,0:T(8,128)(2,1)}, f32[512,128]{1,0:T(8,128)}, f32[128,512]{1,0:T(8,128)}) custom-call(bf16[256,512]{1,0:T(8,128)(2,1)} %get-tuple-element.6.refs_0_, f32[512,128]{1,0:T(8,128)} %get-tuple-element.7.refs_1_, f32[128,512]{1,0:T(8,128)} %get-tuple-element.8.refs_2_), custom_call_target="tpu_custom_call" | custom-call | tf_op jit(solution)/shard_map/pallas_call | solution.py:448

commit v8 on v7

--- a/solution.py
+++ b/solution.py
@@ -40,7 +40,6 @@
     nodes_ref, gin_ref, gout_ref,
     rows_a, rows_c, at, ct, tiles, w_in, w_out, act, gpre, part, chain_out, chain_in, anti_out, fin_in,
     acc, back_out, back_in, halo_out, halo_in, pieces, piece_in, triple, triple_in, total,
-    nodes_buf, gin_buf, gout_buf,
     s_sem, r_sem, l_sem,
 ):
     zg_n = nz // Z_IN
@@ -80,7 +79,7 @@
 
     barrier = pltpu.get_barrier_semaphore()
     peers = [y_fwd, y_bwd, across, mate, along_y(sign, other), along_y(-sign, other)]
-    peers += [along_y(HALF, core), along_y(HALF, other), nxt, prv]
+    peers += [nxt, prv]
     peers += [d for _, d, _ in scatter_peers] + [d for _, d in tri_peers]
     for peer in peers:
         pl.semaphore_signal(barrier, inc=1, device_id=peer, device_id_type=MESH)
@@ -341,9 +340,7 @@
 
     arrive(halo_in.at[0], k_halo)
     arrive(halo_in.at[1], k_halo + 1)
-    nodes_buf[...] = (acc[...] + halo_in[1].astype(F32) + halo_in[0].astype(F32)).astype(BF16)
-    out_nodes = pltpu.make_async_copy(nodes_buf, nodes_ref, l_sem.at[0])
-    out_nodes.start()
+    nodes_ref[...] = (acc[...] + halo_in[1].astype(F32) + halo_in[0].astype(F32)).astype(BF16)
 
     for j, peer in tri_peers:
         arrive(triple_in.at[lax.rem(zg + zg_n - j, zg_n)], k_tri + j)
@@ -360,29 +357,17 @@
     send(total.at[core], total.at[core], k_swap, mate)
     arrive(total.at[other], k_swap)
     for p in range(npiece):
-        gin_buf[p * prow : (p + 1) * prow, :] = total[0, p].astype(F32) * norm_factor
-    out_gin = pltpu.make_async_copy(gin_buf, gin_ref, l_sem.at[1])
-    out_gin.start()
-    gout_buf[...] = jnp.concatenate([total[1, p] for p in range(npiece)], axis=0).T.astype(F32) * norm_factor
-    out_gout = pltpu.make_async_copy(gout_buf, gout_ref, l_sem.at[2])
-    out_gout.start()
+        gin_ref[p * prow : (p + 1) * prow, :] = total[0, p].astype(F32) * norm_factor
+    gout_ref[...] = jnp.concatenate([total[1, p] for p in range(npiece)], axis=0).T.astype(F32) * norm_factor
     for copy in started:
         copy.wait_send()
-    out_nodes.wait()
-    out_gin.wait()
-    out_gout.wait()
 
 
 def hand_over(*refs):
-    n = len(refs) // 3
-    sems = refs[-1]
-    fetch = [pltpu.make_async_copy(refs[k], refs[2 * n + k], sems.at[k]) for k in range(n)]
-    store = [pltpu.make_async_copy(refs[2 * n + k], refs[n + k], sems.at[n + k]) for k in range(n)]
-    for copy in fetch:
+    n = len(refs) // 2
+    store = [pltpu.make_async_copy(refs[k], refs[n + k], refs[-1].at[k]) for k in range(n)]
+    for copy in store:
         copy.start()
-    for k in range(n):
-        fetch[k].wait()
-        store[k].start()
     for copy in store:
         copy.wait()
 
@@ -406,9 +391,9 @@
     )
     results = pl.pallas_call(
         functools.partial(kernel, nz, norm_factor),
-        out_shape=shapes,
+        out_shape=tuple(pltpu.VMEM(s.shape, s.dtype) for s in shapes),
         in_specs=[hbm] * 5 + [scalars] * 2,
-        out_specs=(hbm, hbm, hbm),
+        out_specs=(pl.BlockSpec(memory_space=pltpu.VMEM),) * 3,
         scratch_shapes=[
             vmem((4 * nrow, feat)),
             vmem((4 * nrow, feat)),
@@ -434,24 +419,24 @@
             vmem((prow, hid)),
             vmem((zg_n, prow, hid)),
             vmem((2, npiece, prow, hid)),
-            vmem((nrow, feat)),
-            vmem((feat, hid), F32),
-            vmem((hid, feat), F32),
             pltpu.SemaphoreType.DMA((N_SEM,)),
             pltpu.SemaphoreType.DMA((N_SEM,)),
             pltpu.SemaphoreType.DMA((5,)),
         ],
         compiler_params=pltpu.CompilerParams(
-            collective_id=0, has_side_effects=True, vmem_limit_bytes=62 << 20
+            collective_id=0, has_side_effects=True, vmem_limit_bytes=40 << 20
         ),
-    )(aggregated, cotangent, kernel_in, kernel_out, tile_values, tile_cols, tile_count)
+    )(
+        *[pltpu.with_memory_space_constraint(a, pltpu.HBM) for a in (aggregated, cotangent, kernel_in, kernel_out, tile_values)],
+        tile_cols, tile_count,
+    )
     return pl.pallas_call(
         hand_over,
         out_shape=shapes,
-        in_specs=[hbm] * 3,
+        in_specs=[pl.BlockSpec(memory_space=pltpu.VMEM)] * 3,
         out_specs=(hbm, hbm, hbm),
-        scratch_shapes=[vmem(s.shape, s.dtype) for s in shapes] + [pltpu.SemaphoreType.DMA((6,))],
-        compiler_params=pltpu.CompilerParams(vmem_limit_bytes=62 << 20),
+        scratch_shapes=[pltpu.SemaphoreType.DMA((3,))],
+        compiler_params=pltpu.CompilerParams(vmem_limit_bytes=8 << 20),
     )(*results)
 
 

time: 74.3 us -> 72.2 us (0.972)
  Pallas kernels: 72.8 us -> 70.7 us
    pallas_call x2, Pallas kernels: 72.8 us -> 70.7 us  [the longest x1 69.8 us: local(): pl.pallas_call(functools.partial(kernel, nz, norm_factor), out_shape=tupl...]
where the time goes in v8:
time: 72.2 us; the launch traced here: 72.1 us
  Pallas kernels  70.7 us (98%)
  between operations  1.31 us (2%)
    pallas_call x1, Pallas kernels, local(): pl.pallas_call(functools.partial(kernel, nz, norm_factor), out_shape=tupl...  69.8 us

profile of v8, /device:TPU:1, one launch (start us, length us, event | category | flops | bytes accessed | tf_op | source)
XLA Modules:
  0.0 72.1 jit_solution(16613482764228917088)
XLA Ops:
  0.6 0.0 copy-start
  1.3 0.0 copy-done
  1.3 69.8 %shard_map.94 = (bf16[256,512]{1,0:T(8,128)(2,1)S(1)}, f32[512,128]{1,0:T(8,128)S(1)}, f32[128,512]{1,0:T(8,128)S(1)}) custom-call(bf16[256,512]{1,0:T(8,128)(2,1)} %agg_ref.1, bf16[256,512]{1,0:T(8,128)(2,1)} %cot_ref.1, bf16[512,128]{1,0:T(8,128)(2,1)} %kin_ref.1, bf16[128,512]{1,0:T(8,128)(2,1)} %kout_ref.1, bf16[1,4,256,256]{3,2,1,0:T(8,128)(2,1)} %tiles_ref.1, ...), custom_call_target="tpu_custom_call" | custom-call | tf_op jit(solution)/shard_map/pallas_call | solution.py:392
  71.2 0.9 %shard_map.95 = (bf16[256,512]{1,0:T(8,128)(2,1)}, f32[512,128]{1,0:T(8,128)}, f32[128,512]{1,0:T(8,128)}) custom-call(bf16[256,512]{1,0:T(8,128)(2,1)S(1)} %get-tuple-element.6.refs_0_, f32[512,128]{1,0:T(8,128)S(1)} %get-tuple-element.7.refs_1_, f32[128,512]{1,0:T(8,128)S(1)} %get-tuple-element.8.refs_2_), custom_call_target="tpu_custom_call" | custom-call | tf_op jit(solution)/shard_map/pallas_call | solution.py:433
Async XLA Ops:
  0.6 0.7 copy-start
